TPU v7x, 256 devices: a whole 4x4x8 slice. The times are simulated.
256 devices in a mesh: dp: 2 (over y_lo), ctx: 128 (over y_hi, z, x, core).
Axes of the slice: x: 4, y: 4 (y_hi: 2, y_lo: 2; y = y_hi * 2 + y_lo), z: 8, core: 2. Of those that a mesh axis runs over, the one named last changes fastest.
Arguments:
- features: bfloat16 [2, 256, 512, 512], P('dp', 'ctx'), may hold values from -20 to 20
- w_qkv: bfloat16 [512, 1536], replicated, may hold values from -0.7 to 0.7
- w_out: bfloat16 [512, 512], replicated, may hold values from -0.25 to 0.25
- layout: int32 [4, 4, 4], replicated, may hold values from 0 to 1, as said below
- grad_out: bfloat16 [2, 256, 512, 512], P('dp', 'ctx'), may hold values from -6 to 6
Outputs:
- layer_out: bfloat16 [2, 256, 512, 512], P('dp', 'ctx')
- grad_features: bfloat16 [2, 256, 512, 512], P('dp', 'ctx')
- grad_qkv: float32 [512, 1536], P('ctx')
- grad_wout: float32 [512, 512], P('ctx')
Inputs may be any that keep to these rules, and one draw needn't show every extreme that they name: layout[h, a, b] is 1 where a == b and 0 where b > a.
All inputs are finite; a program needn't handle non-finite values.
Results may differ from a plain program's by a relative error of at most 0.015.
Values may be sent and summed in bfloat16 or wider, within the bound.
A program may use at most 128 MiB of HBM per device.

v0:
```python
import jax
import jax.numpy as jnp
from jax import lax
from jax.sharding import PartitionSpec as P

HEADS = 8
BLOCK = 128


def attend(queries, key_rows, value_rows, d_out, allowed):
    scale_factor = queries.shape[-1] ** (-0.5)
    scores = (
        jnp.einsum("nhid,nhjd->nhij", queries, key_rows, preferred_element_type=jnp.float32)
        * scale_factor
    )
    scores = jnp.where(allowed, scores, jnp.float32(-1e30))
    row_top = jnp.max(scores, axis=-1, keepdims=True)
    weights = jnp.where(allowed, jnp.exp(scores - row_top), jnp.float32(0.0))
    probs = weights / jnp.sum(weights, axis=-1, keepdims=True)
    p_low = probs.astype(jnp.bfloat16)
    attended = jnp.einsum(
        "nhij,nhjd->nhid", p_low, value_rows, preferred_element_type=jnp.float32
    ).astype(jnp.bfloat16)
    d_prob = jnp.einsum("nhid,nhjd->nhij", d_out, value_rows, preferred_element_type=jnp.float32)
    d_score = probs * (d_prob - jnp.sum(probs * d_prob, axis=-1, keepdims=True))
    ds_low = d_score.astype(jnp.bfloat16)
    d_query = (
        jnp.einsum("nhij,nhjd->nhid", ds_low, key_rows, preferred_element_type=jnp.float32)
        * scale_factor
    ).astype(jnp.bfloat16)
    d_key = (
        jnp.einsum("nhij,nhid->nhjd", ds_low, queries, preferred_element_type=jnp.float32)
        * scale_factor
    ).astype(jnp.bfloat16)
    d_value = jnp.einsum(
        "nhij,nhid->nhjd", p_low, d_out, preferred_element_type=jnp.float32
    ).astype(jnp.bfloat16)
    return (attended, d_query, d_key, d_value)


def on_device(features, w_qkv, w_out, layout, grad_out):
    n_clips, n_rows, length, model_width = features.shape
    n_heads = HEADS
    head_size = model_width // n_heads
    row_heads = n_heads // 2
    col_heads = n_heads - row_heads
    total = n_clips * n_rows * length
    flat_in = features.reshape(total, model_width)
    flat_grad = grad_out.reshape(total, model_width)
    projected = jnp.dot(flat_in, w_qkv, preferred_element_type=jnp.float32).astype(jnp.bfloat16)
    projected = projected.reshape(n_clips, n_rows, length, 3, n_heads, head_size)
    d_att = jnp.dot(flat_grad, w_out.T, preferred_element_type=jnp.float32).astype(jnp.bfloat16)
    d_att = d_att.reshape(n_clips, n_rows, length, n_heads, head_size)
    col_proj = projected[:, :, :, :, row_heads:].reshape(
        n_clips, n_rows, length, 3 * col_heads * head_size
    )
    col_dout = d_att[:, :, :, row_heads:].reshape(n_clips, n_rows, length, col_heads * head_size)
    proj_cols = lax.all_to_all(col_proj, "ctx", split_axis=2, concat_axis=1, tiled=True)
    dout_cols = lax.all_to_all(col_dout, "ctx", split_axis=2, concat_axis=1, tiled=True)
    items = proj_cols.shape[0]
    grid = proj_cols.shape[1]
    cols = proj_cols.shape[2]
    proj_six = proj_cols.reshape(items, grid, cols, 3, col_heads, head_size).transpose(
        0, 2, 3, 4, 1, 5
    )
    proj_six = proj_six.reshape(items * cols, 3, col_heads, grid, head_size)
    dout_four = dout_cols.reshape(items, grid, cols, col_heads, head_size).transpose(0, 2, 3, 1, 4)
    dout_four = dout_four.reshape(items * cols, col_heads, grid, head_size)
    grid_pos = jnp.arange(grid)
    allowed = (grid_pos[None, :] <= grid_pos[:, None])[None, None]
    col_att, d_query, d_key, d_value = attend(
        proj_six[:, 0], proj_six[:, 1], proj_six[:, 2], dout_four, allowed
    )
    col_att = col_att.reshape(items, cols, col_heads, grid, head_size).transpose(0, 3, 1, 2, 4)
    col_att = col_att.reshape(items, grid, cols, col_heads * head_size)
    col_grad = jnp.stack([d_query, d_key, d_value], 1).reshape(
        items, cols, 3, col_heads, grid, head_size
    )
    col_grad = col_grad.transpose(0, 4, 1, 2, 3, 5).reshape(
        items, grid, cols, 3 * col_heads * head_size
    )
    col_att_rows = lax.all_to_all(col_att, "ctx", split_axis=1, concat_axis=2, tiled=True)
    col_grad_rows = lax.all_to_all(col_grad, "ctx", split_axis=1, concat_axis=2, tiled=True)
    positions = jnp.arange(length)
    causal = positions[None, :] <= positions[:, None]
    layout_full = jnp.repeat(jnp.repeat(layout, BLOCK, axis=1), BLOCK, axis=2)
    row_allowed = (causal[None] & (layout_full == 1))[None]
    row_in = projected[:, :, :, :, :row_heads].transpose(0, 1, 3, 4, 2, 5)
    row_in = row_in.reshape(n_clips * n_rows, 3, row_heads, length, head_size)
    row_dout = (
        d_att[:, :, :, :row_heads]
        .transpose(0, 1, 3, 2, 4)
        .reshape(n_clips * n_rows, row_heads, length, head_size)
    )
    row_att, d_query, d_key, d_value = attend(
        row_in[:, 0], row_in[:, 1], row_in[:, 2], row_dout, row_allowed
    )
    row_att = row_att.reshape(n_clips, n_rows, row_heads, length, head_size).transpose(
        0, 1, 3, 2, 4
    )
    row_att = row_att.reshape(n_clips, n_rows, length, row_heads * head_size)
    row_grad = jnp.stack([d_query, d_key, d_value], 1).reshape(
        n_clips, n_rows, 3, row_heads, length, head_size
    )
    row_grad = row_grad.transpose(0, 1, 4, 2, 3, 5)
    attended = jnp.concatenate([row_att, col_att_rows], 3).reshape(total, model_width)
    col_grad_six = col_grad_rows.reshape(n_clips, n_rows, length, 3, col_heads, head_size)
    d_proj = jnp.concatenate([row_grad, col_grad_six], 4).reshape(total, 3 * model_width)
    layer_out = jnp.dot(attended, w_out, preferred_element_type=jnp.float32).astype(jnp.bfloat16)
    grad_features = jnp.dot(d_proj, w_qkv.T, preferred_element_type=jnp.float32).astype(
        jnp.bfloat16
    )
    dims = (((0,), (0,)), ((), ()))
    part_qkv = lax.dot_general(flat_in, d_proj, dims, preferred_element_type=jnp.float32)
    part_out = lax.dot_general(attended, flat_grad, dims, preferred_element_type=jnp.float32)
    full_terms = jnp.concatenate([part_qkv, part_out], 1)
    summed_full = lax.psum(full_terms.astype(jnp.bfloat16), "dp").astype(jnp.float32)
    grad_rows = lax.psum_scatter(summed_full, "ctx", scatter_dimension=0, tiled=True)
    grad_qkv = grad_rows[:, : 3 * model_width]
    grad_wout = grad_rows[:, 3 * model_width :]
    shape_local = (n_clips, n_rows, length, model_width)
    return (layer_out.reshape(shape_local), grad_features.reshape(shape_local), grad_qkv, grad_wout)


def solution(mesh):
    return jax.shard_map(
        on_device,
        mesh=mesh,
        in_specs=(P("dp", "ctx", None, None), P(), P(), P(), P("dp", "ctx", None, None)),
        out_specs=(
            P("dp", "ctx", None, None),
            P("dp", "ctx", None, None),
            P("ctx", None),
            P("ctx", None),
        ),
        check_vma=False,
    )
```

profile of v0, /device:TPU:1, one launch (start us, length us, event | category | flops | bytes accessed | tf_op | source)
XLA Modules:
  0.0 1002.8 jit_solution(4845321915034923542)
XLA Ops:
  16.1 16.9 %all-to-all-start.2 = ((bf16[1,2,512,256]{3,1,0,2:T(2,128)(2,1)}), bf16[1,2,512,256]{3,1,0,2:T(2,128)(2,1)}, u32[]{:S(2)}, u32[]{:S(2)}) async-start(bf16[1,2,512,256]{3,1,0,2:T(2,128)(2,1)} %copy.111), calls=%async_computation.2 | async-start | bytes 1048576 | tf_op jit(solution)/shard_map/all_to_all | solution.py:59
  33.0 4.7 convolution_convert_fusion
  37.7 4.6 copy.93
  42.3 6.1 reshape.134
  48.4 3.9 fusion.56
  54.1 4.4 copy.98
  58.5 14.5 %all-to-all-start = ((bf16[1,2,512,768]{3,1,0,2:T(2,128)(2,1)}), bf16[1,2,512,768]{3,1,0,2:T(2,128)(2,1)S(1)}, u32[]{:S(2)}, u32[]{:S(2)}) async-start(bf16[1,2,512,768]{3,1,0,2:T(2,128)(2,1)} %copy.98), calls=%async_computation | async-start | bytes 3145728 | tf_op jit(solution)/shard_map/all_to_all | solution.py:58
  74.5 9.4 fusion.59
  83.9 5.2 fusion.16
  91.2 8.3 multiply_reduce_fusion
  101.5 2.8 reshape.148
  104.3 2.3 copy.113
  106.6 10.5 %all-to-all-done = bf16[1,2,512,768]{3,1,0,2:T(2,128)(2,1)S(1)} async-done(((bf16[1,2,512,768]{3,1,0,2:T(2,128)(2,1)}), bf16[1,2,512,768]{3,1,0,2:T(2,128)(2,1)S(1)}, u32[]{:S(2)}, u32[]{:S(2)}) %all-to-all-start) | async-done | bytes 1572896 | tf_op jit(solution)/shard_map/all_to_all | solution.py:58
  119.0 5.9 reshape.138
  124.9 4.5 copy.100
  133.8 2.8 multiply_reduce_fusion.1
  138.7 6.4 all-to-all-start.1
  145.2 4.3 multiply_convert_fusion.1
  152.9 2.3 copy.118
  155.2 10.4 %all-to-all-done.1 = bf16[1,256,4,256]{3,2,0,1:T(4,128)(2,1)} async-done(((bf16[1,256,4,256]{3,2,0,1:T(4,128)(2,1)}), bf16[1,256,4,256]{3,2,0,1:T(4,128)(2,1)}, u32[]{:S(2)}, u32[]{:S(2)}) %all-to-all-start.1) | async-done | bytes 524320 | tf_op jit(solution)/shard_map/all_to_all | solution.py:82
  165.6 5.5 all-to-all-start.3
  171.2 7.1 multiply_convert_fusion
  180.5 4.8 fusion.31
  190.6 3.1 fusion.15
  193.7 21.8 %all-to-all-done.3 = bf16[1,256,4,768]{3,2,0,1:T(4,128)(2,1)S(1)} async-done(((bf16[1,256,4,768]{3,2,0,1:T(4,128)(2,1)}), bf16[1,256,4,768]{3,2,0,1:T(4,128)(2,1)S(1)}, u32[]{:S(2)}, u32[]{:S(2)}) %all-to-all-start.3) | async-done | bytes 1572896 | tf_op jit(solution)/shard_map/all_to_all | solution.py:83
  217.2 5.9 reshape.152
  223.2 5.8 copy.120
  230.7 3.3 copy.121
  240.8 2.9 convolution_convert_fusion.4
  243.7 2.8 convolution_convert_fusion.2
  246.5 59.0 %all-reduce.4.cloned.1.call-done = bf16[512,2048]{0,1:T(8,128)(2,1)} async-done(((bf16[512,2048]{0,1:T(8,128)(2,1)}), bf16[512,2048]{0,1:T(8,128)(2,1)}) %all-reduce.4.cloned.1.call-update) | async-done | bytes 2097168 | tf_op jit(solution)/shard_map/psum | solution.py:117
  305.5 686.2 %all-reduce.5 = f32[512,2048]{0,1:T(8,128)} all-reduce(bf16[512,2048]{0,1:T(8,128)(2,1)} %all-reduce.4.cloned.1.call-done), channel_id=2, replica_groups=mesh['dp'=2,'ctx'=128] {'ctx'}, use_global_device_ids=true, to_apply=%region_7.8.clone | all-reduce | flops 1048576 | bytes 6291456
  (79 shorter events, 49.0 us)
Async XLA Ops:
  7.2 25.8 %copy-start = (bf16[512,1536]{1,0:T(8,128)(2,1)S(1)}, bf16[512,1536]{1,0:T(8,128)(2,1)}, u32[]{:S(2)}) copy-start(bf16[512,1536]{1,0:T(8,128)(2,1)} %param.6) | copy-start | bytes 4718596
  16.1 42.4 %all-to-all-start.2 = ((bf16[1,2,512,256]{3,1,0,2:T(2,128)(2,1)}), bf16[1,2,512,256]{3,1,0,2:T(2,128)(2,1)}, u32[]{:S(2)}, u32[]{:S(2)}) async-start(bf16[1,2,512,256]{3,1,0,2:T(2,128)(2,1)} %copy.111), calls=%async_computation.2 | async-start | bytes 1048576 | tf_op jit(solution)/shard_map/all_to_all | solution.py:59
  52.3 1.5 copy-start.13
  58.5 58.7 %all-to-all-start = ((bf16[1,2,512,768]{3,1,0,2:T(2,128)(2,1)}), bf16[1,2,512,768]{3,1,0,2:T(2,128)(2,1)S(1)}, u32[]{:S(2)}, u32[]{:S(2)}) async-start(bf16[1,2,512,768]{3,1,0,2:T(2,128)(2,1)} %copy.98), calls=%async_computation | async-start | bytes 3145728 | tf_op jit(solution)/shard_map/all_to_all | solution.py:58
  131.7 2.1 copy-start.4
  131.7 2.1 copy-start.9
  138.7 26.9 %all-to-all-start.1 = ((bf16[1,256,4,256]{3,2,0,1:T(4,128)(2,1)}), bf16[1,256,4,256]{3,2,0,1:T(4,128)(2,1)}, u32[]{:S(2)}, u32[]{:S(2)}) async-start(bf16[1,256,4,256]{3,2,0,1:T(4,128)(2,1)} %copy.102), calls=%async_computation.1 | async-start | bytes 1048576 | tf_op jit(solution)/shard_map/all_to_all | solution.py:82
  149.4 2.2 copy-start.5
  149.4 2.3 copy-start.10
  165.6 49.9 %all-to-all-start.3 = ((bf16[1,256,4,768]{3,2,0,1:T(4,128)(2,1)}), bf16[1,256,4,768]{3,2,0,1:T(4,128)(2,1)S(1)}, u32[]{:S(2)}, u32[]{:S(2)}) async-start(bf16[1,256,4,768]{3,2,0,1:T(4,128)(2,1)} %copy.118), calls=%async_computation.3 | async-start | bytes 3145728 | tf_op jit(solution)/shard_map/all_to_all | solution.py:83
  171.1 134.4 %all-reduce.4.cloned.1.call-start = ((), (), s32[]{:S(2)}) async-start(), calls=%async_computation.4 | async-start | bytes 4194304 | tf_op jit(solution)/shard_map/psum | solution.py:117
  171.1 7.1 copy-start.3
  179.1 1.4 copy-start.11
  223.2 5.8 copy-start.1
  233.9 1.2 copy-start.14
  234.8 2.2 copy-start.6
  235.1 1.8 copy-start.12
  237.0 1.5 copy-start.8
  238.5 0.7 copy-start.15
  238.5 1.9 copy-start.2
  240.7 2.9 copy-start.7
Sparse Core Ops, SparseCore 0:
  238.6 66.7 all-reduce.3
where the time goes:
time: 1020 us; the launch traced here: 1000 us
  blocking collectives  686 us (67%)
  waiting for transfers between devices  102 us (10%)
  local copies, waits for them, and re-layouts  82.8 us (8%)
  matrix products  54.2 us (5%)
  starting transfers between devices  43.3 us (4%)
  other arithmetic  19.1 us (2%)
  between operations  15.3 us (2%)
    unnamed x1, blocking collectives  686 us
    psum x1, waiting for transfers between devices, on_device(): lax.psum(full_terms.astype(jnp.bfloat16), 'dp').astype(jnp.float32)  59 us
    all_to_all x1, waiting for transfers between devices, on_device(): lax.all_to_all(col_grad, 'ctx', split_axis=1, concat_axis=2, tiled=True)  21.8 us
  transfers between devices with their start and end apart: 5, of which 4 were waited for; matrix products, arithmetic and copies ran while one was open for 10% of the time, Pallas kernels for 0%

commit v1 on v0

v1 whole, which is shorter than its diff:
```python
import functools

import jax
import jax.numpy as jnp
from jax import lax
from jax.experimental import pallas as pl
from jax.experimental.pallas import tpu as pltpu
from jax.sharding import PartitionSpec as P

HEADS = 8
HEAD = 64
BLOCK = 128
HALF = 256
SCALE = HEAD**-0.5
NEG = -1e30
BF = jnp.bfloat16
F32 = jnp.float32
VMEM_LIMIT = 56 * 1024 * 1024


def nn(a, b):
    return jnp.dot(a, b, preferred_element_type=F32)


def nt(a, b):
    return lax.dot_general(a, b, (((1,), (1,)), ((), ())), preferred_element_type=F32)


def eye(n):
    r = lax.broadcasted_iota(jnp.int32, (n, n), 0)
    c = lax.broadcasted_iota(jnp.int32, (n, n), 1)
    return (r == c).astype(F32).astype(BF)


def turned(x, ident):
    return nt(ident, x).astype(BF)


def wire_matrix():
    t = lax.broadcasted_iota(jnp.int32, (256, 256), 0)
    k = lax.broadcasted_iota(jnp.int32, (256, 256), 1)
    src = ((t >> 2) & 1) * 128 + (t >> 3) * 4 + (t & 3)
    return (k == src).astype(F32).astype(BF)


def unwire_matrix():
    t = lax.broadcasted_iota(jnp.int32, (256, 256), 1)
    k = lax.broadcasted_iota(jnp.int32, (256, 256), 0)
    src = ((t >> 2) & 1) * 128 + (t >> 3) * 4 + (t & 3)
    return (k == src).astype(F32).astype(BF)


def column_matrix():
    t = lax.broadcasted_iota(jnp.int32, (256, 256), 0)
    k = lax.broadcasted_iota(jnp.int32, (256, 256), 1)
    return (k == (t & 63) * 4 + (t >> 6)).astype(F32).astype(BF)


def uncolumn_matrix():
    t = lax.broadcasted_iota(jnp.int32, (256, 256), 1)
    k = lax.broadcasted_iota(jnp.int32, (256, 256), 0)
    return (k == (t & 63) * 4 + (t >> 6)).astype(F32).astype(BF)


def rows_of_head(x, h):
    r = lax.broadcasted_iota(jnp.int32, x.shape, 0)
    return jnp.where((r >> 6) == h, x, jnp.zeros_like(x))


def lanes_of_head(x, h):
    c = lax.broadcasted_iota(jnp.int32, x.shape, 1)
    return jnp.where((c >> 6) == h, x, jnp.zeros_like(x))


def attend_head(h, k_all, v_all, k_t, v_t, q_t, d_t, q_all, d_all, mask):
    scores = nn(k_all, rows_of_head(q_t, h)) * SCALE
    scores = jnp.where(mask, scores, NEG)
    top = jnp.max(scores, axis=0, keepdims=True)
    weights = jnp.exp(scores - top)
    probs = weights * (1.0 / jnp.sum(weights, axis=0, keepdims=True))
    p_low = probs.astype(BF)
    out_t = nn(v_t[h * HEAD : (h + 1) * HEAD], p_low)
    d_prob = nn(v_all, rows_of_head(d_t, h))
    delta = jnp.sum(probs * d_prob, axis=0, keepdims=True)
    ds_low = (probs * (d_prob - delta)).astype(BF)
    dq_t = nn(k_t[h * HEAD : (h + 1) * HEAD], ds_low) * SCALE
    dv = nn(p_low, lanes_of_head(d_all, h))
    dk = nn(ds_low, lanes_of_head(q_all, h))
    return out_t, dq_t, dk, dv


def to_wire_kernel(x_ref, o_ref):
    perm = wire_matrix()
    for b in range(4):
        x = jnp.concatenate(
            [x_ref[128 * b : 128 * b + 128], x_ref[512 + 128 * b : 512 + 128 * b + 128]], 0
        )
        o_ref[256 * b : 256 * b + 256] = nn(perm, x).astype(BF)


def dout_kernel(g_ref, w_ref, o_ref):
    perm = wire_matrix()
    for b in range(4):
        x = jnp.concatenate(
            [g_ref[128 * b : 128 * b + 128], g_ref[512 + 128 * b : 512 + 128 * b + 128]], 0
        )
        d = nt(x, w_ref[HALF:]).astype(BF)
        o_ref[256 * b : 256 * b + 256] = nn(perm, d).astype(BF)


def row_kernel(lay_ref, f_ref, g_ref, w_ref, wo_ref, att_ref, gf_ref, gq_ref, gwo_ref, dk_ref, dv_ref):
    step = pl.program_id(0)
    feats = f_ref[0]
    grads = g_ref[0]
    n = feats.shape[0]
    ident = eye(256)
    wq, wk, wv = (w_ref[:, s * 512 : s * 512 + HALF] for s in range(3))
    q_all = nn(feats, wq).astype(BF)
    k_all = nn(feats, wk).astype(BF)
    v_all = nn(feats, wv).astype(BF)
    d_all = nt(grads, wo_ref[:HALF]).astype(BF)
    q_t, k_t, v_t, d_t = (turned(x, ident) for x in (q_all, k_all, v_all, d_all))
    dk_ref[...] = jnp.zeros_like(dk_ref)
    dv_ref[...] = jnp.zeros_like(dv_ref)
    att_parts, dq_parts = [], []
    width = 256
    for chunk in range(n // width):
        nj = (chunk + 1) * width
        cols = slice(chunk * width, (chunk + 1) * width)
        key = lax.broadcasted_iota(jnp.int32, (nj, width), 0)
        qry = lax.broadcasted_iota(jnp.int32, (nj, width), 1) + chunk * width
        causal = key <= qry
        lane = lax.broadcasted_iota(jnp.int32, (1, width), 1)
        outs, dqs = [], []
        for h in range(4):
            tiles = []
            for jb in range(nj // BLOCK):
                line = jnp.where(
                    lane < BLOCK, lay_ref[h, 2 * chunk, jb], lay_ref[h, 2 * chunk + 1, jb]
                )
                tiles.append(jnp.broadcast_to(line, (BLOCK, width)))
            mask = jnp.logical_and(causal, jnp.concatenate(tiles, 0) == 1)
            out_t, dq_t, dk, dv = attend_head(
                h, k_all[:nj], v_all[:nj], k_t[:, :nj], v_t[:, :nj],
                q_t[:, cols], d_t[:, cols], q_all[cols], d_all[cols], mask,
            )
            dk_ref[:nj] += dk
            dv_ref[:nj] += dv
            outs.append(out_t)
            dqs.append(dq_t)
        att_parts.append(jnp.concatenate(outs, 0).astype(BF))
        dq_parts.append(jnp.concatenate(dqs, 0).astype(BF))
    att_t = jnp.concatenate(att_parts, 1)
    dq_tt = jnp.concatenate(dq_parts, 1)
    att_ref[0] = jnp.concatenate([nt(ident, p) for p in att_parts], 0).astype(BF)
    dq = jnp.concatenate([nt(ident, p) for p in dq_parts], 0).astype(BF)
    del dq_tt
    dk = (dk_ref[...] * SCALE).astype(BF)
    dv = dv_ref[...].astype(BF)
    gf_ref[0] = nt(dq, wq) + nt(dk, wk) + nt(dv, wv)
    feats_t = jnp.concatenate([turned(feats[:, :256], ident), turned(feats[:, 256:], ident)], 0)

    @pl.when(step == 0)
    def _():
        gq_ref[...] = jnp.zeros_like(gq_ref)
        gwo_ref[...] = jnp.zeros_like(gwo_ref)

    for s, d in enumerate((dq, dk, dv)):
        gq_ref[:, s * HALF : (s + 1) * HALF] += nn(feats_t, d)
    gwo_ref[...] += nn(att_t, grads)


def col_kernel(f_ref, d_ref, w_ref, att_ref, gf_ref, gq_ref, fcol, dcol, acol, gcol):
    ident = eye(256)
    perm = column_matrix()
    for b in range(4):
        rows = slice(256 * b, 256 * b + 256)
        x = nn(perm, f_ref[rows]).astype(BF)
        d = nn(perm, d_ref[rows]).astype(BF)
        for c in range(4):
            fcol[c, 64 * b : 64 * b + 64] = x[64 * c : 64 * c + 64]
            dcol[c, 64 * b : 64 * b + 64] = d[64 * c : 64 * c + 64]
    wq, wk, wv = (w_ref[:, s * 512 + HALF : s * 512 + 512] for s in range(3))
    key = lax.broadcasted_iota(jnp.int32, (256, 256), 0)
    qry = lax.broadcasted_iota(jnp.int32, (256, 256), 1)
    mask = key <= qry
    gq_ref[...] = jnp.zeros_like(gq_ref)

    @pl.loop(0, 4)
    def _(c):
        feats = fcol[c]
        q_all = nn(feats, wq).astype(BF)
        k_all = nn(feats, wk).astype(BF)
        v_all = nn(feats, wv).astype(BF)
        d_all = dcol[c]
        q_t, k_t, v_t, d_t = (turned(x, ident) for x in (q_all, k_all, v_all, d_all))
        outs, dqs, dk, dv = [], [], None, None
        for h in range(4):
            out_t, dq_t, dk_h, dv_h = attend_head(
                h, k_all, v_all, k_t, v_t, q_t, d_t, q_all, d_all, mask
            )
            outs.append(out_t)
            dqs.append(dq_t)
            dk = dk_h if dk is None else dk + dk_h
            dv = dv_h if dv is None else dv + dv_h
        att = nt(ident, jnp.concatenate(outs, 0).astype(BF)).astype(BF)
        dq = nt(ident, jnp.concatenate(dqs, 0).astype(BF)).astype(BF)
        dk = (dk * SCALE).astype(BF)
        dv = dv.astype(BF)
        acol[c] = att
        gcol[c] = (nt(dq, wq) + nt(dk, wk) + nt(dv, wv)).astype(BF)
        feats_t = jnp.concatenate([turned(feats[:, :256], ident), turned(feats[:, 256:], ident)], 0)
        for s, d in enumerate((dq, dk, dv)):
            gq_ref[:, s * HALF : (s + 1) * HALF] += nn(feats_t, d)

    back = uncolumn_matrix()
    for b in range(4):
        rows = slice(256 * b, 256 * b + 256)
        a = jnp.concatenate([acol[c, 64 * b : 64 * b + 64] for c in range(4)], 0)
        g = jnp.concatenate([gcol[c, 64 * b : 64 * b + 64] for c in range(4)], 0)
        att_ref[rows] = nn(back, a).astype(BF)
        gf_ref[rows] = nn(back, g).astype(BF)


def out_kernel(arow_ref, awire_ref, g_ref, wo_ref, out_ref, gwo_ref):
    perm = unwire_matrix()
    ident = eye(256)
    gwo = None
    for b in range(4):
        a = nn(perm, awire_ref[256 * b : 256 * b + 256]).astype(BF)
        pieces = []
        for r in range(2):
            rows = slice(512 * r + 128 * b, 512 * r + 128 * b + 128)
            col = a[128 * r : 128 * r + 128]
            out_ref[rows] = (nn(arow_ref[rows], wo_ref[:HALF]) + nn(col, wo_ref[HALF:])).astype(BF)
            pieces.append(g_ref[rows])
        term = nn(turned(a, ident), jnp.concatenate(pieces, 0))
        gwo = term if gwo is None else gwo + term
    gwo_ref[...] = gwo


def gf_kernel(gf_ref, gwire_ref, out_ref):
    perm = unwire_matrix()
    for b in range(4):
        g = nn(perm, gwire_ref[256 * b : 256 * b + 256])
        for r in range(2):
            rows = slice(512 * r + 128 * b, 512 * r + 128 * b + 128)
            out_ref[rows] = (gf_ref[rows] + g[128 * r : 128 * r + 128]).astype(BF)


def scatter_kernel(n_y, n_z, n_x, g_ref, o_ref, cbuf, a_buf, xbuf, b_buf, ybuf, d_buf, zbuf, e_buf, lbuf,
                   ssem, csem, xsem, ysem, zsem, lsem):
    dp = lax.axis_index("dp")
    ctx = lax.axis_index("ctx")
    core = ctx % 2
    x = (ctx // 2) % n_x
    z = (ctx // (2 * n_x)) % n_z
    yh = ctx // (2 * n_x * n_z)
    half = g_ref.shape[-1] // 2

    def dev(yh_, z_, x_, core_, dp_):
        return (dp_, ((yh_ * n_z + z_) * n_x + x_) * 2 + core_)

    mate = dev(yh, z, x, 1 - core, dp)
    x_peers = [dev(yh, z, (x + s) % n_x, core, dp) for s in range(1, n_x)]
    y_peers = [((yh + s // 2) % 2, (dp + s) % 2) for s in range(1, 4)]
    z_peers = [(z + s) % n_z for s in range(1, n_z)]
    everyone = (
        [mate]
        + x_peers
        + [dev(a, z, x, core, b) for a, b in y_peers]
        + [dev(yh, a, x, core, dp) for a in z_peers]
    )
    barrier = pltpu.get_barrier_semaphore()
    for d in everyone:
        pl.semaphore_signal(barrier, inc=1, device_id=d, device_id_type=pl.DeviceIdType.MESH)
    pl.semaphore_wait(barrier, len(everyone))

    def remote(src, dst, s, r, d):
        return pltpu.make_async_remote_copy(
            src_ref=src, dst_ref=dst, send_sem=s, recv_sem=r, device_id=d,
            device_id_type=pl.DeviceIdType.MESH,
        )

    copy = remote(g_ref.at[:, :, :, :, pl.ds(pl.multiple_of((1 - core) * half, 128), half)], cbuf,
                  ssem.at[0], csem.at[0], mate)
    copy.start()
    copy.wait()
    mine = pl.ds(pl.multiple_of(core * half, 128), half)
    for zz in range(n_z):
        a_buf[:, :, zz] = (
            g_ref[:, zz, :, :, mine].astype(F32) + cbuf[:, zz].astype(F32)
        ).astype(BF).swapaxes(0, 1)
    copies = []
    for s in range(1, n_x):
        to = (x + s) % n_x
        copies.append(remote(a_buf.at[to], xbuf.at[s - 1], ssem.at[s], xsem.at[s - 1],
                             dev(yh, z, to, core, dp)))
    for c in copies:
        c.start()
    for c in copies:
        c.wait()
    for yy in range(n_y):
        total = a_buf[x, yy].astype(F32)
        for s in range(1, n_x):
            total = total + xbuf[s - 1, yy].astype(F32)
        b_buf[yy] = total.astype(BF)
    here = yh * 2 + dp
    copies = []
    for s in range(1, 4):
        to = (here + s) % 4
        copies.append(remote(b_buf.at[to // 2], ybuf.at[here], ssem.at[3 + s], ysem.at[s - 1],
                             dev(to // 2, z, x, core, to % 2)))
    for c in copies:
        c.start()
    ybuf[here] = b_buf[yh]
    for c in copies:
        c.wait()
    total = ybuf[0].astype(F32)
    for s in range(1, 4):
        total = total + ybuf[s].astype(F32)
    d_buf[...] = total.astype(BF)
    copies = []
    for s in range(1, n_z):
        to = (z + s) % n_z
        copies.append(remote(d_buf.at[to], zbuf.at[z], ssem.at[6 + s], zsem.at[s - 1],
                             dev(yh, to, x, core, dp)))
    for c in copies:
        c.start()
    zbuf[z] = d_buf[z]
    for c in copies:
        c.wait()
    total = zbuf[0].astype(F32)
    for s in range(1, n_z):
        total = total + zbuf[s].astype(F32)
    e_buf[...] = total
    copy = remote(e_buf, lbuf, ssem.at[7 + n_z - 1], lsem.at[0], mate)
    copy.start()
    copy.wait()
    own, other = e_buf[...], lbuf[...]
    first = jnp.where(core == 0, own, other)
    second = jnp.where(core == 0, other, own)
    full = jnp.concatenate([first, second], 1)
    o_ref[...] = jnp.where(core == 0, full[:4], full[4:])


def scatter_sum(g, cid):
    rows, cols = g.shape
    n_y, n_z, n_x, half = 2, 8, 4, cols // 2
    g = g.reshape(n_y, n_z, n_x, 8, cols)
    vm = pl.BlockSpec(memory_space=pltpu.VMEM)
    sem = pltpu.SemaphoreType.DMA
    return pl.pallas_call(
        functools.partial(scatter_kernel, n_y, n_z, n_x),
        out_shape=jax.ShapeDtypeStruct((4, cols), F32),
        in_specs=[vm],
        out_specs=vm,
        scratch_shapes=[
            pltpu.VMEM((n_y, n_z, n_x, 8, half), BF),
            pltpu.VMEM((n_x, n_y, n_z, 8, half), BF),
            pltpu.VMEM((n_x - 1, n_y, n_z, 8, half), BF),
            pltpu.VMEM((n_y, n_z, 8, half), BF),
            pltpu.VMEM((4, n_z, 8, half), BF),
            pltpu.VMEM((n_z, 8, half), BF),
            pltpu.VMEM((n_z, 8, half), BF),
            pltpu.VMEM((8, half), F32),
            pltpu.VMEM((8, half), F32),
            sem((7 + n_z,)),
            sem((1,)),
            sem((n_x - 1,)),
            sem((3,)),
            sem((n_z - 1,)),
            sem((1,)),
        ],
        compiler_params=pltpu.CompilerParams(
            collective_id=cid, has_side_effects=True, vmem_limit_bytes=VMEM_LIMIT
        ),
        cost_estimate=pl.CostEstimate(flops=rows * cols, bytes_accessed=8 * rows * cols, transcendentals=0),
        name="scatter_sum",
    )(g)


def call(kernel, outs, *args, scratch=(), cost=1_000_000, name=None):
    return pl.pallas_call(
        kernel,
        out_shape=[jax.ShapeDtypeStruct(s, d) for s, d in outs],
        scratch_shapes=list(scratch),
        compiler_params=pltpu.CompilerParams(vmem_limit_bytes=VMEM_LIMIT),
        cost_estimate=pl.CostEstimate(flops=cost, bytes_accessed=4_000_000, transcendentals=0),
        name=name,
    )(*args)


def row_part(features, grad_out, w_qkv, w_out, layout):
    n = features.shape[0]
    whole = lambda *shape: pl.BlockSpec(shape, lambda r: (0,) * len(shape))
    per_row = lambda *shape: pl.BlockSpec((1,) + shape, lambda r: (r, 0, 0))
    return pl.pallas_call(
        row_kernel,
        grid=(n,),
        in_specs=[
            pl.BlockSpec(memory_space=pltpu.SMEM),
            per_row(512, 512),
            per_row(512, 512),
            whole(512, 1536),
            whole(512, 512),
        ],
        out_specs=[per_row(512, 256), per_row(512, 512), whole(512, 768), whole(256, 512)],
        out_shape=[
            jax.ShapeDtypeStruct((n, 512, 256), BF),
            jax.ShapeDtypeStruct((n, 512, 512), F32),
            jax.ShapeDtypeStruct((512, 768), F32),
            jax.ShapeDtypeStruct((256, 512), F32),
        ],
        scratch_shapes=[pltpu.VMEM((512, 256), F32), pltpu.VMEM((512, 256), F32)],
        compiler_params=pltpu.CompilerParams(
            dimension_semantics=("arbitrary",), vmem_limit_bytes=VMEM_LIMIT
        ),
        cost_estimate=pl.CostEstimate(
            flops=12_000_000_000, bytes_accessed=12_000_000, transcendentals=2_000_000
        ),
        name="row_heads",
    )(layout, features, grad_out, w_qkv, w_out)


def col_part(f_got, d_got, w_qkv):
    return call(
        col_kernel,
        [((1024, 256), BF), ((1024, 512), BF), ((512, 768), F32)],
        f_got, d_got, w_qkv,
        scratch=[
            pltpu.VMEM((4, 256, 512), BF),
            pltpu.VMEM((4, 256, 256), BF),
            pltpu.VMEM((4, 256, 256), BF),
            pltpu.VMEM((4, 256, 512), BF),
        ],
        cost=6_000_000_000,
        name="col_heads",
    )


def on_device(features, w_qkv, w_out, layout, grad_out):
    n_clips, n_rows, length, width = features.shape
    total = n_clips * n_rows * length
    n_ctx = lax.axis_size("ctx")
    feats = features.reshape(total, width)
    grads = grad_out.reshape(total, width)

    def swap(x):
        x = x.reshape(n_ctx, total // n_ctx, x.shape[-1])
        x = lax.all_to_all(x, "ctx", split_axis=0, concat_axis=0, tiled=True)
        return x.reshape(total, x.shape[-1])

    (f_wire,) = call(to_wire_kernel, [((total, width), BF)], feats, name="to_wire")
    f_got = swap(f_wire)
    (d_wire,) = call(dout_kernel, [((total, HALF), BF)], grads, w_out, name="dout")
    d_got = swap(d_wire)
    att_row, gf_row, gq_row, gwo_row = row_part(
        features.reshape(n_rows, length, width), grad_out.reshape(n_rows, length, width),
        w_qkv, w_out, layout,
    )
    att_wire, gf_wire, gq_col = col_part(f_got, d_got, w_qkv)
    att_got = swap(att_wire)
    gf_got = swap(gf_wire)
    layer_out, gwo_col = call(
        out_kernel, [((total, width), BF), ((HALF, width), F32)],
        att_row.reshape(total, HALF), att_got, grads, w_out, name="home_out",
    )
    (grad_features,) = call(
        gf_kernel, [((total, width), BF)], gf_row.reshape(total, width), gf_got, name="home_gf"
    )
    gq = jnp.stack([gq_row.reshape(512, 3, HALF), gq_col.reshape(512, 3, HALF)], 2)
    terms = jnp.concatenate([gq.reshape(512, 1536), jnp.concatenate([gwo_row, gwo_col], 0)], 1)
    rows = scatter_sum(terms.astype(BF), 1)
    shape = (n_clips, n_rows, length, width)
    return layer_out.reshape(shape), grad_features.reshape(shape), rows[:, :1536], rows[:, 1536:]


def solution(mesh):
    return jax.shard_map(
        on_device,
        mesh=mesh,
        in_specs=(P("dp", "ctx", None, None), P(), P(), P(), P("dp", "ctx", None, None)),
        out_specs=(
            P("dp", "ctx", None, None),
            P("dp", "ctx", None, None),
            P("ctx", None),
            P("ctx", None),
        ),
        check_vma=False,
    )
```

time: 1020 us -> 221 us (0.22); the launches traced: 1000 us -> 220 us
  blocking collectives: 686 us -> 67.3 us
  Pallas kernels: 0 us -> 96.9 us
  waiting for transfers between devices: 102 us -> 19.4 us
  local copies, waits for them, and re-layouts: 82.8 us -> 5.88 us
  matrix products: 54.2 us -> 0 us
  starting transfers between devices: 43.3 us -> 23.1 us
  between operations: 15.3 us -> 0.72 us
  other arithmetic: 19.1 us -> 6.92 us
    unnamed x1 -> x0, blocking collectives: 686 us -> none
    pallas_call x0 -> x7, Pallas kernels: none -> 96.9 us  [the longest x1 41 us: scatter_sum(): pl.pallas_call(functools.partial(scatter_kernel, n_y, n_z, n_x), out_shap...]
    all_to_all x0 -> x2, blocking collectives: none -> 67.3 us  [swap(): x = lax.all_to_all(x, 'ctx', split_axis=0, concat_axis=0, tiled=True)]
    psum x1 -> x0, waiting for transfers between devices: 59 us -> none  [on_device(): lax.psum(full_terms.astype(jnp.bfloat16), 'dp').astype(jnp.float32)]
    reshape x13 -> x0, local copies, waits for them, and re-layouts: 48.1 us -> none  [the longest x2 11.7 us: on_device(): col_grad_rows.reshape(n_clips, n_rows, length, 3, col_heads, head_size)]
    dot_general x17 -> x0, matrix products: 44.8 us -> none  [the longest x2 11.1 us: attend(): jnp.einsum('nhid,nhjd->nhij', d_out, value_rows, preferred_element_type=j...]
    all_to_all x4 -> x2, waiting for transfers between devices: 42.8 us -> 19.4 us  [swap(): x = lax.all_to_all(x, 'ctx', split_axis=0, concat_axis=0, tiled=True)]
    all_to_all x4 -> x2, starting transfers between devices: 43.3 us -> 23.1 us  [swap(): x = lax.all_to_all(x, 'ctx', split_axis=0, concat_axis=0, tiled=True)]
  transfers between devices with their start and end apart: 5 -> 2, of which waited for: 4 -> 1; matrix products, arithmetic and copies ran while one was open for 10% -> 6% of each run, Pallas kernels for 0% -> 32%
where the time goes in v1:
time: 221 us; the launch traced here: 220 us
  Pallas kernels  96.9 us (44%)
  blocking collectives  67.3 us (30%)
  starting transfers between devices  23.1 us (10%)
  waiting for transfers between devices  19.4 us (9%)
  other arithmetic  6.92 us (3%)
  local copies, waits for them, and re-layouts  5.88 us (3%)
    all_to_all x2, blocking collectives, swap(): x = lax.all_to_all(x, 'ctx', split_axis=0, concat_axis=0, tiled=True)  67.3 us
    pallas_call x1, Pallas kernels, scatter_sum(): pl.pallas_call(functools.partial(scatter_kernel, n_y, n_z, n_x), out_shap...  41 us
    pallas_call x5, Pallas kernels, call(): pl.pallas_call(kernel, out_shape=[jax.ShapeDtypeStruct(s, d) for s, d in...  34.3 us
    all_to_all x2, starting transfers between devices, swap(): x = lax.all_to_all(x, 'ctx', split_axis=0, concat_axis=0, tiled=True)  23.1 us
    pallas_call x1, Pallas kernels, row_part(): pl.pallas_call(row_kernel, grid=(n,), in_specs=[pl.BlockSpec(memory_space...  21.5 us
    all_to_all x2, waiting for transfers between devices, swap(): x = lax.all_to_all(x, 'ctx', split_axis=0, concat_axis=0, tiled=True)  19.4 us
    another operation x4, other arithmetic  5.12 us
  transfers between devices with their start and end apart: 2, of which 1 were waited for; matrix products, arithmetic and copies ran while one was open for 6% of the time, Pallas kernels for 32%

profile of v1, /device:TPU:1, one launch (start us, length us, event | category | flops | bytes accessed | tf_op | source)
XLA Modules:
  0.0 220.2 jit_solution(6899927042949213450)
XLA Ops:
  0.6 3.4 %dout.1 = bf16[1024,256]{1,0:T(8,128)(2,1)} custom-call(bf16[1024,512]{1,0:T(8,128)(2,1)} %bitcast.19, bf16[512,512]{1,0:T(8,128)(2,1)} %wo_ref.3), custom_call_target="tpu_custom_call" | custom-call | flops 1000000 | bytes 4000000 | tf_op jit(solution)/shard_map/dout/pallas_call | solution.py:384
  4.1 16.4 %all-to-all-start.1 = ((bf16[128,8,256]{2,1,0:T(8,128)(2,1)}), bf16[128,8,256]{2,1,0:T(8,128)(2,1)S(1)}, u32[]{:S(2)}, u32[]{:S(2)}) async-start(bf16[128,8,256]{2,1,0:T(8,128)(2,1)} %bitcast.27), calls=%async_computation.1 | async-start | bytes 1048576 | tf_op jit(solution)/shard_map/all_to_all | solution.py:451
  20.5 2.6 %to_wire.1 = bf16[1024,512]{1,0:T(8,128)(2,1)} custom-call(bf16[1024,512]{1,0:T(8,128)(2,1)} %bitcast.29), custom_call_target="tpu_custom_call" | custom-call | flops 1000000 | bytes 4000000 | tf_op jit(solution)/shard_map/to_wire/pallas_call | solution.py:384
  23.1 19.4 %all-to-all-done.1 = bf16[128,8,256]{2,1,0:T(8,128)(2,1)S(1)} async-done(((bf16[128,8,256]{2,1,0:T(8,128)(2,1)}), bf16[128,8,256]{2,1,0:T(8,128)(2,1)S(1)}, u32[]{:S(2)}, u32[]{:S(2)}) %all-to-all-start.1) | async-done | bytes 524320 | tf_op jit(solution)/shard_map/all_to_all | solution.py:451
  42.5 0.0 copy-start
  42.5 39.6 %all_to_all.20 = bf16[128,8,512]{2,1,0:T(8,128)(2,1)} all-to-all(bf16[128,8,512]{2,1,0:T(8,128)(2,1)} %bitcast.22), channel_id=1, replica_groups=mesh['dp'=2,'ctx'=128] {'ctx'}, dimensions={0} | all-to-all | bytes 2097152 | tf_op jit(solution)/shard_map/all_to_all | solution.py:451
  82.2 0.0 copy-done
  82.2 20.6 %col_heads.1 = (bf16[1024,256]{1,0:T(8,128)(2,1)}, bf16[1024,512]{1,0:T(8,128)(2,1)}, f32[512,768]{1,0:T(8,128)}) custom-call(bf16[1024,512]{1,0:T(8,128)(2,1)} %bitcast.32, bf16[1024,256]{1,0:T(8,128)(2,1)} %bitcast.35, bf16[512,1536]{1,0:T(8,128)(2,1)} %w_ref.5), custom_call_target="tpu_custom_call" | custom-call | flops 6000000000 | bytes 4000000 | tf_op jit(solution)/shard_map/col_heads/pallas_call | solution.py:384
  102.7 27.7 %all_to_all.21 = bf16[128,8,256]{2,1,0:T(8,128)(2,1)} all-to-all(bf16[128,8,256]{2,1,0:T(8,128)(2,1)} %bitcast.36), channel_id=1, replica_groups=mesh['dp'=2,'ctx'=128] {'ctx'}, dimensions={0} | all-to-all | bytes 1048576 | tf_op jit(solution)/shard_map/all_to_all | solution.py:451
  130.4 6.7 %all-to-all-start.3 = ((bf16[128,8,512]{2,1,0:T(8,128)(2,1)}), bf16[128,8,512]{2,1,0:T(8,128)(2,1)}, u32[]{:S(2)}, u32[]{:S(2)}) async-start(bf16[128,8,512]{2,1,0:T(8,128)(2,1)} %bitcast.31), calls=%async_computation.3 | async-start | bytes 2097152 | tf_op jit(solution)/shard_map/all_to_all | solution.py:451
  137.1 21.5 %row_heads.1 = (bf16[2,512,256]{2,1,0:T(8,128)(2,1)}, f32[2,512,512]{2,1,0:T(8,128)}, f32[512,768]{1,0:T(8,128)}, f32[256,512]{1,0:T(8,128)}) custom-call(s32[4,4,4]{2,1,0:T(4,128)} %lay_ref.1, bf16[2,512,512]{2,1,0:T(8,128)(2,1)} %bitcast.30, bf16[2,512,512]{2,1,0:T(8,128)(2,1)} %bitcast.20, bf16[512,1536]{1,0:T(8,128)(2,1)} %w_ref.5, bf16[512,512]{1,0:T(8,128)(2,1)} %wo_ref.3), custom_call_target="tpu_custom_call" | custom-call | flops 12000000000 | bytes 12000000 | tf_op jit(solution)/shard_map/row_heads/pallas_call | solution.py:398
  158.6 1.1 convert.20
  159.7 1.5 convert.18
  161.2 0.3 copy.11
  161.5 1.5 convert.19
  163.0 0.3 copy.12
  163.3 0.1 pad_maximum_fusion.1
  163.4 1.6 copy.13
  165.1 1.0 concatenate.13
  166.1 4.4 %home_out.1 = (bf16[1024,512]{1,0:T(8,128)(2,1)}, f32[256,512]{1,0:T(8,128)}) custom-call(bf16[1024,256]{1,0:T(8,128)(2,1)} %bitcast.34, bf16[1024,256]{1,0:T(8,128)(2,1)} %bitcast.25, bf16[1024,512]{1,0:T(8,128)(2,1)} %bitcast.21, bf16[512,512]{1,0:T(8,128)(2,1)} %wo_ref.3), custom_call_target="tpu_custom_call" | custom-call | flops 1000000 | bytes 4000000 | tf_op jit(solution)/shard_map/home_out/pallas_call | solution.py:384
  170.6 1.1 convert.21
  171.7 1.6 pad_maximum_fusion.g_ref
  173.3 41.0 %scatter_sum.1 = f32[4,2048]{1,0:T(4,128)} custom-call(bf16[2,8,4,8,2048]{4,3,2,1,0:T(8,128)(2,1)} %pad_maximum_fusion.g_ref), custom_call_target="tpu_custom_call" | custom-call | flops 1048576 | bytes 8388608 | tf_op jit(solution)/shard_map/scatter_sum/pallas_call | solution.py:353
  214.3 1.3 slice.7
  215.6 1.3 slice.6
  217.0 0.0 all-to-all-done.3
  217.0 3.3 %home_gf.1 = bf16[1024,512]{1,0:T(8,128)(2,1)} custom-call(f32[1024,512]{1,0:T(8,128)} %bitcast.26, bf16[1024,512]{1,0:T(8,128)(2,1)} %bitcast.14.gwire_ref), custom_call_target="tpu_custom_call" | custom-call | flops 1000000 | bytes 4000000 | tf_op jit(solution)/shard_map/home_gf/pallas_call | solution.py:384
  (1 shorter events, 0.0 us)
Async XLA Ops:
  4.1 38.5 %all-to-all-start.1 = ((bf16[128,8,256]{2,1,0:T(8,128)(2,1)}), bf16[128,8,256]{2,1,0:T(8,128)(2,1)S(1)}, u32[]{:S(2)}, u32[]{:S(2)}) async-start(bf16[128,8,256]{2,1,0:T(8,128)(2,1)} %bitcast.27), calls=%async_computation.1 | async-start | bytes 1048576 | tf_op jit(solution)/shard_map/all_to_all | solution.py:451
  42.5 39.6 %copy-start = (bf16[128,8,256]{2,1,0:T(8,128)(2,1)}, bf16[128,8,256]{2,1,0:T(8,128)(2,1)S(1)}, u32[]{:S(2)}) copy-start(bf16[128,8,256]{2,1,0:T(8,128)(2,1)S(1)} %all-to-all-done.1) | copy-start | bytes 1572868
  130.4 86.6 %all-to-all-start.3 = ((bf16[128,8,512]{2,1,0:T(8,128)(2,1)}), bf16[128,8,512]{2,1,0:T(8,128)(2,1)}, u32[]{:S(2)}, u32[]{:S(2)}) async-start(bf16[128,8,512]{2,1,0:T(8,128)(2,1)} %bitcast.31), calls=%async_computation.3 | async-start | bytes 2097152 | tf_op jit(solution)/shard_map/all_to_all | solution.py:451

commit v2 on v0

v2 whole, which is shorter than its diff:
```python
import functools

import jax
import jax.numpy as jnp
from jax import lax
from jax.experimental import pallas as pl
from jax.experimental.pallas import tpu as pltpu
from jax.sharding import PartitionSpec as P

HEADS = 8
HEAD = 64
BLOCK = 128
HALF = 256
SCALE = HEAD**-0.5
NEG = -1e30
BF = jnp.bfloat16
F32 = jnp.float32
VMEM_LIMIT = 58 * 1024 * 1024
MESH = pl.DeviceIdType.MESH
N_Y, N_Z, N_X = 2, 8, 4


def nn(a, b):
    return jnp.dot(a, b, preferred_element_type=F32)


def nt(a, b):
    return lax.dot_general(a, b, (((1,), (1,)), ((), ())), preferred_element_type=F32)


def eye(n):
    r = lax.broadcasted_iota(jnp.int32, (n, n), 0)
    c = lax.broadcasted_iota(jnp.int32, (n, n), 1)
    return (r == c).astype(F32).astype(BF)


def turned(x, ident):
    return nt(ident, x).astype(BF)


def wire_matrix():
    t = lax.broadcasted_iota(jnp.int32, (256, 256), 0)
    k = lax.broadcasted_iota(jnp.int32, (256, 256), 1)
    src = ((t >> 2) & 1) * 128 + (t >> 3) * 4 + (t & 3)
    return (k == src).astype(F32).astype(BF)


def unwire_matrix():
    t = lax.broadcasted_iota(jnp.int32, (256, 256), 1)
    k = lax.broadcasted_iota(jnp.int32, (256, 256), 0)
    src = ((t >> 2) & 1) * 128 + (t >> 3) * 4 + (t & 3)
    return (k == src).astype(F32).astype(BF)


def column_matrix():
    t = lax.broadcasted_iota(jnp.int32, (256, 256), 0)
    k = lax.broadcasted_iota(jnp.int32, (256, 256), 1)
    return (k == (t & 63) * 4 + (t >> 6)).astype(F32).astype(BF)


def uncolumn_matrix():
    t = lax.broadcasted_iota(jnp.int32, (256, 256), 1)
    k = lax.broadcasted_iota(jnp.int32, (256, 256), 0)
    return (k == (t & 63) * 4 + (t >> 6)).astype(F32).astype(BF)


def rows_of_head(x, h):
    r = lax.broadcasted_iota(jnp.int32, x.shape, 0)
    return jnp.where((r >> 6) == h, x, jnp.zeros_like(x))


def lanes_of_head(x, h):
    c = lax.broadcasted_iota(jnp.int32, x.shape, 1)
    return jnp.where((c >> 6) == h, x, jnp.zeros_like(x))


def softmax_t(scores, mask):
    scores = jnp.where(mask, scores * SCALE, NEG)
    top = jnp.max(scores, axis=0, keepdims=True)
    weights = jnp.exp(scores - top)
    return weights * (1.0 / jnp.sum(weights, axis=0, keepdims=True))


def score_grad(probs, d_prob):
    delta = jnp.sum(probs * d_prob, axis=0, keepdims=True)
    return (probs * (d_prob - delta)).astype(BF)


def head_rows(h):
    return slice(h * HEAD, (h + 1) * HEAD)


class Place:
    def __init__(self):
        self.dp = lax.axis_index("dp")
        self.ctx = lax.axis_index("ctx")
        self.core = self.ctx % 2
        self.x = (self.ctx // 2) % N_X
        self.z = (self.ctx // (2 * N_X)) % N_Z
        self.yh = self.ctx // (2 * N_X * N_Z)

    def at(self, yh=None, z=None, x=None, core=None, dp=None):
        yh = self.yh if yh is None else yh
        z = self.z if z is None else z
        x = self.x if x is None else x
        core = self.core if core is None else core
        dp = self.dp if dp is None else dp
        return (dp, ((yh * N_Z + z) * N_X + x) * 2 + core)


def remote(src, dst, send, recv, device):
    return pltpu.make_async_remote_copy(
        src_ref=src, dst_ref=dst, send_sem=send, recv_sem=recv, device_id=device, device_id_type=MESH
    )


class Scatter:
    def __init__(self, place, g, bufs, sems):
        self.place, self.g = place, g
        self.c, self.a, self.xb, self.b, self.yb, self.d, self.zb, self.e, self.last = bufs
        self.send, self.cs, self.xs, self.ys, self.zs, self.ls = sems
        self.half = g.shape[-1] // 2
        self.copies = []

    def launch(self, copies):
        for c in copies:
            c.start()
        self.copies = copies

    def arrive(self):
        for c in self.copies:
            c.wait()

    def to_core(self):
        p, half = self.place, self.half
        theirs = pl.ds(pl.multiple_of((1 - p.core) * half, 128), half)
        self.launch([
            remote(self.g.at[:, :, :, :, theirs], self.c, self.send.at[0], self.cs.at[0],
                   p.at(core=1 - p.core))
        ])

    def to_x(self):
        p, half = self.place, self.half
        self.arrive()
        mine = pl.ds(pl.multiple_of(p.core * half, 128), half)

        @pl.loop(0, N_Z)
        def _(zz):
            for yy in range(N_Y):
                self.a[:, yy, zz] = (
                    self.g[yy, zz, :, :, mine].astype(F32) + self.c[yy, zz].astype(F32)
                ).astype(BF)

        copies = []
        for s in range(1, N_X):
            to = (p.x + s) % N_X
            copies.append(remote(self.a.at[to], self.xb.at[s - 1], self.send.at[s],
                                 self.xs.at[s - 1], p.at(x=to)))
        self.launch(copies)

    def to_y(self):
        p = self.place
        self.arrive()

        @pl.loop(0, N_Y)
        def _(yy):
            total = self.a[p.x, yy].astype(F32)
            for s in range(N_X - 1):
                total = total + self.xb[s, yy].astype(F32)
            self.b[yy] = total.astype(BF)

        here = p.yh * 2 + p.dp
        copies = []
        for s in range(1, 4):
            to = (here + s) % 4
            copies.append(remote(self.b.at[to // 2], self.yb.at[here], self.send.at[3 + s],
                                 self.ys.at[s - 1], p.at(yh=to // 2, dp=to % 2)))
        self.launch(copies)
        self.yb[here] = self.b[p.yh]

    def to_z(self):
        p = self.place
        self.arrive()
        total = self.yb[0].astype(F32)
        for s in range(1, 4):
            total = total + self.yb[s].astype(F32)
        self.d[...] = total.astype(BF)
        copies = []
        for s in range(1, N_Z):
            to = (p.z + s) % N_Z
            copies.append(remote(self.d.at[to], self.zb.at[p.z], self.send.at[6 + s],
                                 self.zs.at[s - 1], p.at(z=to)))
        self.launch(copies)
        self.zb[p.z] = self.d[p.z]

    def to_mate(self):
        p = self.place
        self.arrive()
        total = self.zb[0].astype(F32)
        for s in range(1, N_Z):
            total = total + self.zb[s].astype(F32)
        self.e[...] = total
        self.launch([
            remote(self.e, self.last, self.send.at[6 + N_Z], self.ls.at[0], p.at(core=1 - p.core))
        ])

    def result(self):
        self.arrive()
        first = self.place.core == 0
        own, other = self.e[...], self.last[...]
        full = jnp.concatenate([jnp.where(first, own, other), jnp.where(first, other, own)], 1)
        return jnp.where(first, full[:4], full[4:])


def scatter_scratch(cols):
    half = cols // 2
    sem = pltpu.SemaphoreType.DMA
    bufs = [
        pltpu.VMEM((N_Y, N_Z, N_X, 8, half), BF),
        pltpu.VMEM((N_X, N_Y, N_Z, 8, half), BF),
        pltpu.VMEM((N_X - 1, N_Y, N_Z, 8, half), BF),
        pltpu.VMEM((N_Y, N_Z, 8, half), BF),
        pltpu.VMEM((4, N_Z, 8, half), BF),
        pltpu.VMEM((N_Z, 8, half), BF),
        pltpu.VMEM((N_Z, 8, half), BF),
        pltpu.VMEM((8, half), F32),
        pltpu.VMEM((8, half), F32),
    ]
    sems = [sem((7 + N_Z,)), sem((1,)), sem((N_X - 1,)), sem((3,)), sem((N_Z - 1,)), sem((1,))]
    return dict(g=pltpu.VMEM((N_Y, N_Z, N_X, 8, cols), BF), bufs=bufs, sems=sems)


class Swap:
    def __init__(self, place, src, dst, send, recv):
        self.place, self.src, self.dst, self.send, self.recv = place, src, dst, send, recv
        self.n = src.shape[0]

    def start(self):
        p, n = self.place, self.n

        def step(s, carry):
            to = (p.ctx + s) % n
            remote(self.src.at[to], self.dst.at[p.ctx], self.send, self.recv, (p.dp, to)).start()
            return carry

        lax.fori_loop(1, n, step, 0)
        self.dst[p.ctx] = self.src[p.ctx]

    def all_but_one(self, ref, sem):
        part = ref.at[pl.ds(0, self.n - 1)]
        pltpu.make_async_copy(part, part, sem).wait()

    def arrived(self):
        self.all_but_one(self.dst, self.recv)

    def gone(self):
        self.all_but_one(self.src, self.send)


def to_wire(ref, get, perm):
    for b in range(4):
        x = get(b)
        y = nn(perm, x).astype(BF)
        ref[32 * b : 32 * b + 32] = y.reshape(32, 8, y.shape[-1])


def block_of(ref, b):
    return jnp.concatenate([ref[r, 128 * b : 128 * b + 128] for r in range(2)], 0)


def to_columns(wire, col, perm):
    for b in range(4):
        x = wire[32 * b : 32 * b + 32]
        y = nn(perm, x.reshape(256, x.shape[-1])).astype(BF)
        for c in range(4):
            col[c, 64 * b : 64 * b + 64] = y[64 * c : 64 * c + 64]


def from_columns(col, wire, perm):
    for b in range(4):
        x = jnp.concatenate([col[c, 64 * b : 64 * b + 64] for c in range(4)], 0)
        y = nn(perm, x).astype(BF)
        wire[32 * b : 32 * b + 32] = y.reshape(32, 8, y.shape[-1])


def turned_wide(x, ident):
    return jnp.concatenate([turned(x[:, :256], ident), turned(x[:, 256:], ident)], 0)


def row_heads(s, r, lay, feats, grads, w, wo, ident):
    n = feats.shape[0]
    wq, wk, wv = (w[:, i * 512 : i * 512 + HALF] for i in range(3))
    q_all = nn(feats, wq).astype(BF)
    k_all = nn(feats, wk).astype(BF)
    v_all = nn(feats, wv).astype(BF)
    d_all = nt(grads, wo[:HALF]).astype(BF)
    q_t, k_t, v_t, d_t = (turned(x, ident) for x in (q_all, k_all, v_all, d_all))
    s["dk"][...] = jnp.zeros_like(s["dk"])
    s["dv"][...] = jnp.zeros_like(s["dv"])
    att_parts, dq_parts = [], []
    width = 256
    for chunk in range(n // width):
        nj = (chunk + 1) * width
        cols = slice(chunk * width, (chunk + 1) * width)
        key = lax.broadcasted_iota(jnp.int32, (nj, width), 0)
        qry = lax.broadcasted_iota(jnp.int32, (nj, width), 1) + chunk * width
        causal = key <= qry
        lane = lax.broadcasted_iota(jnp.int32, (1, width), 1)
        outs, dqs = [], []
        for h in range(4):
            tiles = []
            for jb in range(nj // BLOCK):
                line = jnp.where(lane < BLOCK, lay[h, 2 * chunk, jb], lay[h, 2 * chunk + 1, jb])
                tiles.append(jnp.broadcast_to(line, (BLOCK, width)))
            mask = jnp.logical_and(causal, jnp.concatenate(tiles, 0) == 1)
            probs = softmax_t(nn(k_all[:nj], rows_of_head(q_t[:, cols], h)), mask)
            p_low = probs.astype(BF)
            outs.append(nn(v_t[head_rows(h), :nj], p_low))
            ds_low = score_grad(probs, nn(v_all[:nj], rows_of_head(d_t[:, cols], h)))
            dqs.append(nn(k_t[head_rows(h), :nj], ds_low) * SCALE)
            s["dv"][:nj] += nn(p_low, lanes_of_head(d_all[cols], h))
            s["dk"][:nj] += nn(ds_low, lanes_of_head(q_all[cols], h))
        att_parts.append(jnp.concatenate(outs, 0).astype(BF))
        dq_parts.append(jnp.concatenate(dqs, 0).astype(BF))
    s["att_row"][r] = jnp.concatenate([nt(ident, p) for p in att_parts], 0).astype(BF)
    dq = jnp.concatenate([nt(ident, p) for p in dq_parts], 0).astype(BF)
    dk = (s["dk"][...] * SCALE).astype(BF)
    dv = s["dv"][...].astype(BF)
    s["gf_row"][r] = nt(dq, wq) + nt(dk, wk) + nt(dv, wv)
    feats_t = turned_wide(feats, ident)
    for i, d in enumerate((dq, dk, dv)):
        s["gq_acc"][:, i * HALF : (i + 1) * HALF] += nn(feats_t, d)
    s["gwo_acc"][...] += nn(jnp.concatenate(att_parts, 1), grads)


def put_gq(s, offset):
    for i in range(3):
        part = s["gq_acc"][:, i * HALF : (i + 1) * HALF].astype(BF)
        s["gq"]["g"][:, :, :, :, i * 512 + offset : i * 512 + offset + HALF] = part.reshape(
            N_Y, N_Z, N_X, 8, HALF
        )


def put_gwo(s, half):
    part = s["gwo_acc"][...].astype(BF)
    s["gwo"]["g"][half] = part.reshape(N_Z, N_X, 8, 512)


def whole_kernel(lay, feats, grads, w, wo, out, gf_out, gq_out, gwo_out, s):
    p = Place()
    n_ctx = s["f_wire"].shape[0]
    barrier = pltpu.get_barrier_semaphore()

    def greet(step, carry):
        pl.semaphore_signal(
            barrier, inc=1, device_id=(p.dp, (p.ctx + step) % n_ctx), device_id_type=MESH
        )
        return carry

    lax.fori_loop(1, n_ctx, greet, 0)
    for yh in (p.yh, 1 - p.yh):
        pl.semaphore_signal(barrier, inc=1, device_id=p.at(yh=yh, dp=1 - p.dp), device_id_type=MESH)

    perm = wire_matrix()
    to_wire(s["f_wire"], lambda b: block_of(feats, b), perm)
    pl.semaphore_wait(barrier, n_ctx + 1)
    sems = s["swap"]
    f_swap = Swap(p, s["f_wire"], s["f_got"], sems.at[0], sems.at[1])
    d_swap = Swap(p, s["d_wire"], s["d_got"], sems.at[2], sems.at[3])
    a_swap = Swap(p, s["a_wire"], s["a_got"], sems.at[4], sems.at[5])
    g_swap = Swap(p, s["g_wire"], s["g_got"], sems.at[6], sems.at[7])
    f_swap.start()
    to_wire(s["d_wire"], lambda b: nt(block_of(grads, b), wo[HALF:]).astype(BF), perm)
    d_swap.start()

    ident = eye(256)
    s["gq_acc"][...] = jnp.zeros_like(s["gq_acc"])
    s["gwo_acc"][...] = jnp.zeros_like(s["gwo_acc"])

    @pl.loop(0, 2)
    def _(r):
        row_heads(s, r, lay, feats[r], grads[r], w, wo, ident)

    put_gq(s, 0)
    put_gwo(s, 0)

    key = lax.broadcasted_iota(jnp.int32, (256, 256), 0)
    qry = lax.broadcasted_iota(jnp.int32, (256, 256), 1)
    mask = key <= qry
    wq, wk, wv = (w[:, i * 512 + HALF : i * 512 + 512] for i in range(3))
    split, join = column_matrix(), uncolumn_matrix()
    f_swap.arrived()
    to_columns(s["f_got"], s["f_col"], split)

    @pl.loop(0, 4)
    def _(c):
        x = s["f_col"][c]
        q_all = nn(x, wq).astype(BF)
        k_all = nn(x, wk).astype(BF)
        v_all = nn(x, wv).astype(BF)
        s["q"][c], s["k"][c], s["v"][c] = q_all, k_all, v_all
        q_t, v_t = turned(q_all, ident), turned(v_all, ident)
        outs = []
        for h in range(4):
            probs = softmax_t(nn(k_all, rows_of_head(q_t, h)), mask)
            s["probs"][c, h] = probs
            outs.append(nn(v_t[head_rows(h)], probs.astype(BF)))
        s["a_col"][c] = nt(ident, jnp.concatenate(outs, 0).astype(BF)).astype(BF)

    from_columns(s["a_col"], s["a_wire"], join)
    a_swap.start()

    d_swap.arrived()
    to_columns(s["d_got"], s["d_col"], split)
    s["gq_acc"][...] = jnp.zeros_like(s["gq_acc"])

    @pl.loop(0, 4)
    def _(c):
        x = s["f_col"][c]
        q_all, k_all, v_all, d_all = s["q"][c], s["k"][c], s["v"][c], s["d_col"][c]
        k_t, d_t = turned(k_all, ident), turned(d_all, ident)
        dqs, dk, dv = [], None, None
        for h in range(4):
            probs = s["probs"][c, h]
            ds_low = score_grad(probs, nn(v_all, rows_of_head(d_t, h)))
            dqs.append(nn(k_t[head_rows(h)], ds_low) * SCALE)
            dv_h = nn(probs.astype(BF), lanes_of_head(d_all, h))
            dk_h = nn(ds_low, lanes_of_head(q_all, h))
            dk = dk_h if dk is None else dk + dk_h
            dv = dv_h if dv is None else dv + dv_h
        dq = nt(ident, jnp.concatenate(dqs, 0).astype(BF)).astype(BF)
        dk = (dk * SCALE).astype(BF)
        dv = dv.astype(BF)
        s["g_col"][c] = (nt(dq, wq) + nt(dk, wk) + nt(dv, wv)).astype(BF)
        x_t = turned_wide(x, ident)
        for i, d in enumerate((dq, dk, dv)):
            s["gq_acc"][:, i * HALF : (i + 1) * HALF] += nn(x_t, d)

    from_columns(s["g_col"], s["g_wire"], join)
    g_swap.start()
    put_gq(s, HALF)
    gq = Scatter(p, s["gq"]["g"], s["gq"]["bufs"], s["gq"]["sems"])
    gwo = Scatter(p, s["gwo"]["g"], s["gwo"]["bufs"], s["gwo"]["sems"])
    gq.to_core()

    unwire = unwire_matrix()
    a_swap.arrived()
    s["gwo_acc"][...] = jnp.zeros_like(s["gwo_acc"])
    for b in range(4):
        x = s["a_got"][32 * b : 32 * b + 32]
        a = nn(unwire, x.reshape(256, HALF)).astype(BF)
        s["gwo_acc"][...] += nn(turned(a, ident), block_of(grads, b))
        s["att_col"][0, 128 * b : 128 * b + 128] = a[:128]
        s["att_col"][1, 128 * b : 128 * b + 128] = a[128:]
    put_gwo(s, 1)
    gwo.to_core()
    gq.to_x()
    for r in range(2):
        out[r] = (nn(s["att_row"][r], wo[:HALF]) + nn(s["att_col"][r], wo[HALF:])).astype(BF)
    gwo.to_x()
    gq.to_y()
    gwo.to_y()
    gq.to_z()
    gwo.to_z()
    gq.to_mate()
    gwo.to_mate()
    gq_out[...] = gq.result()
    gwo_out[...] = gwo.result()

    g_swap.arrived()
    for b in range(4):
        x = s["g_got"][32 * b : 32 * b + 32]
        g = nn(unwire, x.reshape(256, 512))
        for r in range(2):
            rows = slice(128 * b, 128 * b + 128)
            gf_out[r, rows] = (s["gf_row"][r, rows] + g[128 * r : 128 * r + 128]).astype(BF)
    for swap in (f_swap, d_swap, a_swap, g_swap):
        swap.gone()


def on_device(features, w_qkv, w_out, layout, grad_out):
    n_clips, n_rows, length, width = features.shape
    n_ctx = lax.axis_size("ctx")
    vm = pl.BlockSpec(memory_space=pltpu.VMEM)
    vmem = pltpu.VMEM
    scratch = dict(
        f_wire=vmem((n_ctx, 8, 512), BF),
        f_got=vmem((n_ctx, 8, 512), BF),
        d_wire=vmem((n_ctx, 8, 256), BF),
        d_got=vmem((n_ctx, 8, 256), BF),
        a_wire=vmem((n_ctx, 8, 256), BF),
        a_got=vmem((n_ctx, 8, 256), BF),
        g_wire=vmem((n_ctx, 8, 512), BF),
        g_got=vmem((n_ctx, 8, 512), BF),
        swap=pltpu.SemaphoreType.DMA((8,)),
        dk=vmem((512, 256), F32),
        dv=vmem((512, 256), F32),
        att_row=vmem((2, 512, 256), BF),
        att_col=vmem((2, 512, 256), BF),
        gf_row=vmem((2, 512, 512), F32),
        gq_acc=vmem((512, 768), F32),
        gwo_acc=vmem((256, 512), F32),
        f_col=vmem((4, 256, 512), BF),
        d_col=vmem((4, 256, 256), BF),
        a_col=vmem((4, 256, 256), BF),
        g_col=vmem((4, 256, 512), BF),
        q=vmem((4, 256, 256), BF),
        k=vmem((4, 256, 256), BF),
        v=vmem((4, 256, 256), BF),
        probs=vmem((4, 4, 256, 256), F32),
        gq=scatter_scratch(1536),
        gwo=scatter_scratch(512),
    )
    flat, tree = jax.tree.flatten(scratch, is_leaf=lambda x: not isinstance(x, (dict, list)))
    n_out = 4

    def kernel(lay, feats, grads, w, wo, *rest):
        outs, refs = rest[:n_out], rest[n_out:]
        whole_kernel(lay, feats, grads, w, wo, *outs, jax.tree.unflatten(tree, refs))

    shape = (n_rows, length, width)
    out, gf, gq, gwo = pl.pallas_call(
        kernel,
        out_shape=[
            jax.ShapeDtypeStruct(shape, BF),
            jax.ShapeDtypeStruct(shape, BF),
            jax.ShapeDtypeStruct((4, 1536), F32),
            jax.ShapeDtypeStruct((4, 512), F32),
        ],
        in_specs=[pl.BlockSpec(memory_space=pltpu.SMEM), vm, vm, vm, vm],
        out_specs=[vm] * n_out,
        scratch_shapes=flat,
        compiler_params=pltpu.CompilerParams(
            collective_id=1, has_side_effects=True, vmem_limit_bytes=VMEM_LIMIT
        ),
        name="whole_layer",
    )(layout, features.reshape(shape), grad_out.reshape(shape), w_qkv, w_out)
    full = (n_clips,) + shape
    return out.reshape(full), gf.reshape(full), gq, gwo


def solution(mesh):
    return jax.shard_map(
        on_device,
        mesh=mesh,
        in_specs=(P("dp", "ctx", None, None), P(), P(), P(), P("dp", "ctx", None, None)),
        out_specs=(
            P("dp", "ctx", None, None),
            P("dp", "ctx", None, None),
            P("ctx", None),
            P("ctx", None),
        ),
        check_vma=False,
    )
```

time: 1020 us -> 111 us (0.11); the launches traced: 1000 us -> 111 us
  blocking collectives: 686 us -> 0 us
  Pallas kernels: 0 us -> 106 us
  waiting for transfers between devices: 102 us -> 0 us
  local copies, waits for them, and re-layouts: 82.8 us -> 4.54 us
  matrix products: 54.2 us -> 0 us
  starting transfers between devices: 43.3 us -> 0 us
  other arithmetic: 19.1 us -> 0 us
  between operations: 15.3 us -> 0.66 us
    unnamed x1 -> x0, blocking collectives: 686 us -> none
    pallas_call x0 -> x1, Pallas kernels: none -> 106 us  [on_device(): pl.pallas_call(kernel, out_shape=[jax.ShapeDtypeStruct(shape, BF), jax.Sh...]
    psum x1 -> x0, waiting for transfers between devices: 59 us -> none  [on_device(): lax.psum(full_terms.astype(jnp.bfloat16), 'dp').astype(jnp.float32)]
    reshape x13 -> x0, local copies, waits for them, and re-layouts: 48.1 us -> none  [the longest x2 11.7 us: on_device(): col_grad_rows.reshape(n_clips, n_rows, length, 3, col_heads, head_size)]
    dot_general x17 -> x0, matrix products: 44.8 us -> none  [the longest x2 11.1 us: attend(): jnp.einsum('nhid,nhjd->nhij', d_out, value_rows, preferred_element_type=j...]
    all_to_all x4 -> x0, starting transfers between devices: 43.3 us -> none  [the longest x1 16.9 us: on_device(): lax.all_to_all(col_dout, 'ctx', split_axis=2, concat_axis=1, tiled=True)]
    all_to_all x4 -> x0, waiting for transfers between devices: 42.8 us -> none  [the longest x1 21.8 us: on_device(): lax.all_to_all(col_grad, 'ctx', split_axis=1, concat_axis=2, tiled=True)]
    convert_element_type x2 -> x0, other arithmetic: 11.4 us -> none  [attend(): ds_low = d_score.astype(jnp.bfloat16)]
  transfers between devices with their start and end apart: 5 -> 0, of which waited for: 4 -> 0; matrix products, arithmetic and copies ran while one was open for 10% -> 0% of each run, Pallas kernels for 0% -> 0%
where the time goes in v2:
time: 111 us
  Pallas kernels  106 us (95%)
  local copies, waits for them, and re-layouts  4.54 us (4%)
    pallas_call x1, Pallas kernels, on_device(): pl.pallas_call(kernel, out_shape=[jax.ShapeDtypeStruct(shape, BF), jax.Sh...  106 us
    unnamed x10, local copies, waits for them, and re-layouts  4.54 us

profile of v2, /device:TPU:1, one launch (start us, length us, event | category | flops | bytes accessed | tf_op | source)
XLA Modules:
  0.0 111.1 jit_solution(14387910159518038717)
XLA Ops:
  0.6 105.9 %whole_layer.1 = (bf16[2,512,512]{2,1,0:T(8,128)(2,1)}, bf16[2,512,512]{2,1,0:T(8,128)(2,1)}, f32[4,1536]{1,0:T(4,128)}, f32[4,512]{1,0:T(4,128)}) custom-call(s32[4,4,4]{2,1,0:T(4,128)} %lay.1, bf16[2,512,512]{2,1,0:T(8,128)(2,1)} %bitcast.6, bf16[2,512,512]{2,1,0:T(8,128)(2,1)} %bitcast.7, bf16[512,1536]{1,0:T(8,128)(2,1)} %w.1, bf16[512,512]{1,0:T(8,128)(2,1)} %wo.1), custom_call_target="tpu_custom_call" | custom-call | tf_op jit(solution)/shard_map/whole_layer/pallas_call | solution.py:522
  106.6 0.0 copy-start
  106.6 0.0 copy-start.1
  106.6 2.3 %copy.13 = bf16[1,2,512,512]{3,2,1,0:T(8,128)(2,1)} copy(bf16[1,2,512,512]{3,2,1,0:T(8,128)(2,1)} %bitcast.5) | data formatting | bytes 2097152
  109.0 0.0 copy-done
  109.0 0.0 copy-start.2
  109.0 1.0 copy.14
  109.9 0.0 copy-done.1
  109.9 0.6 copy.15
  110.5 0.0 copy-done.2
  110.5 0.6 copy.16
Async XLA Ops:
  106.6 2.4 %copy-start = (bf16[2,512,512]{2,1,0:T(8,128)(2,1)S(1)}, bf16[2,512,512]{2,1,0:T(8,128)(2,1)}, u32[]{:S(2)}) copy-start(bf16[2,512,512]{2,1,0:T(8,128)(2,1)} %get-tuple-element.9) | copy-start | bytes 3145732
  106.6 3.3 %copy-start.1 = (f32[4,1536]{1,0:T(4,128)S(1)}, f32[4,1536]{1,0:T(4,128)}, u32[]{:S(2)}) copy-start(f32[4,1536]{1,0:T(4,128)} %get-tuple-element.18) | copy-start | bytes 73732
  109.0 1.6 %copy-start.2 = (f32[4,512]{1,0:T(4,128)S(1)}, f32[4,512]{1,0:T(4,128)}, u32[]{:S(2)}) copy-start(f32[4,512]{1,0:T(4,128)} %get-tuple-element.19) | copy-start | bytes 24580

commit v3 on v2

--- a/solution.py
+++ b/solution.py
@@ -18,6 +18,7 @@
 VMEM_LIMIT = 58 * 1024 * 1024
 MESH = pl.DeviceIdType.MESH
 N_Y, N_Z, N_X = 2, 8, 4
+SCALE_LOG2E = SCALE * 1.4426950408889634
 
 
 def nn(a, b):
@@ -64,26 +65,40 @@
     return (k == (t & 63) * 4 + (t >> 6)).astype(F32).astype(BF)
 
 
-def rows_of_head(x, h):
-    r = lax.broadcasted_iota(jnp.int32, x.shape, 0)
-    return jnp.where((r >> 6) == h, x, jnp.zeros_like(x))
-
-
 def lanes_of_head(x, h):
     c = lax.broadcasted_iota(jnp.int32, x.shape, 1)
     return jnp.where((c >> 6) == h, x, jnp.zeros_like(x))
 
 
-def softmax_t(scores, mask):
-    scores = jnp.where(mask, scores * SCALE, NEG)
-    top = jnp.max(scores, axis=0, keepdims=True)
-    weights = jnp.exp(scores - top)
-    return weights * (1.0 / jnp.sum(weights, axis=0, keepdims=True))
-
-
-def score_grad(probs, d_prob):
-    delta = jnp.sum(probs * d_prob, axis=0, keepdims=True)
-    return (probs * (d_prob - delta)).astype(BF)
+def soften(pieces):
+    high = pieces[0]
+    for x in pieces[1:]:
+        high = jnp.maximum(high, x)
+    top = jnp.max(high, axis=0, keepdims=True)
+    return [jnp.exp2((x - top) * SCALE_LOG2E).astype(BF) for x in pieces]
+
+
+def stacked(pieces, n_keys):
+    rest = n_keys - BLOCK * len(pieces)
+    if rest:
+        pieces = pieces + [jnp.zeros((rest, BLOCK), BF)]
+    return jnp.concatenate(pieces, 0)
+
+
+def padded(x, h):
+    parts = [jnp.zeros((HEAD * h, x.shape[1]), BF)] if h else []
+    parts.append(x)
+    if h < 3:
+        parts.append(jnp.zeros((HEAD * (3 - h), x.shape[1]), BF))
+    return jnp.concatenate(parts, 0)
+
+
+def with_ones(v_t):
+    return jnp.concatenate([v_t, jnp.ones((16, v_t.shape[1]), BF)], 0)
+
+
+def by_head(x):
+    return jnp.concatenate([lanes_of_head(x, h) for h in range(4)], 0)
 
 
 def head_rows(h):
@@ -287,63 +302,130 @@
     return jnp.concatenate([turned(x[:, :256], ident), turned(x[:, 256:], ident)], 0)
 
 
+def side_by_side(w, offset):
+    return jnp.concatenate([w[:, i * 512 + offset : i * 512 + offset + HALF] for i in range(3)], 1)
+
+
 def row_heads(s, r, lay, feats, grads, w, wo, ident):
     n = feats.shape[0]
-    wq, wk, wv = (w[:, i * 512 : i * 512 + HALF] for i in range(3))
-    q_all = nn(feats, wq).astype(BF)
-    k_all = nn(feats, wk).astype(BF)
-    v_all = nn(feats, wv).astype(BF)
-    d_all = nt(grads, wo[:HALF]).astype(BF)
-    q_t, k_t, v_t, d_t = (turned(x, ident) for x in (q_all, k_all, v_all, d_all))
-    s["dk"][...] = jnp.zeros_like(s["dk"])
-    s["dv"][...] = jnp.zeros_like(s["dv"])
-    att_parts, dq_parts = [], []
-    width = 256
+    qkv = nn(feats, w).astype(BF)
+    q_all, k_all, v_all = (qkv[:, i * HALF : (i + 1) * HALF] for i in range(3))
+    d_t = nt(wo[:HALF], grads).astype(BF).astype(F32)
+    q_t, k_t, v_t = (turned(x, ident) for x in (q_all, k_all, v_all))
+    tri = lax.broadcasted_iota(jnp.int32, (BLOCK, BLOCK), 0) <= lax.broadcasted_iota(
+        jnp.int32, (BLOCK, BLOCK), 1
+    )
+    chunks = []
+    width = 2 * BLOCK
     for chunk in range(n // width):
         nj = (chunk + 1) * width
         cols = slice(chunk * width, (chunk + 1) * width)
-        key = lax.broadcasted_iota(jnp.int32, (nj, width), 0)
-        qry = lax.broadcasted_iota(jnp.int32, (nj, width), 1) + chunk * width
-        causal = key <= qry
-        lane = lax.broadcasted_iota(jnp.int32, (1, width), 1)
-        outs, dqs = [], []
+        weights, ds_all, outs, dqs, dts_all = [], [], [], [], []
         for h in range(4):
-            tiles = []
-            for jb in range(nj // BLOCK):
-                line = jnp.where(lane < BLOCK, lay[h, 2 * chunk, jb], lay[h, 2 * chunk + 1, jb])
-                tiles.append(jnp.broadcast_to(line, (BLOCK, width)))
-            mask = jnp.logical_and(causal, jnp.concatenate(tiles, 0) == 1)
-            probs = softmax_t(nn(k_all[:nj], rows_of_head(q_t[:, cols], h)), mask)
-            p_low = probs.astype(BF)
-            outs.append(nn(v_t[head_rows(h), :nj], p_low))
-            ds_low = score_grad(probs, nn(v_all[:nj], rows_of_head(d_t[:, cols], h)))
-            dqs.append(nn(k_t[head_rows(h), :nj], ds_low) * SCALE)
-            s["dv"][:nj] += nn(p_low, lanes_of_head(d_all[cols], h))
-            s["dk"][:nj] += nn(ds_low, lanes_of_head(q_all[cols], h))
-        att_parts.append(jnp.concatenate(outs, 0).astype(BF))
-        dq_parts.append(jnp.concatenate(dqs, 0).astype(BF))
-    s["att_row"][r] = jnp.concatenate([nt(ident, p) for p in att_parts], 0).astype(BF)
-    dq = jnp.concatenate([nt(ident, p) for p in dq_parts], 0).astype(BF)
-    dk = (s["dk"][...] * SCALE).astype(BF)
-    dv = s["dv"][...].astype(BF)
-    s["gf_row"][r] = nt(dq, wq) + nt(dk, wk) + nt(dv, wv)
-    feats_t = turned_wide(feats, ident)
-    for i, d in enumerate((dq, dk, dv)):
-        s["gq_acc"][:, i * HALF : (i + 1) * HALF] += nn(feats_t, d)
-    s["gwo_acc"][...] += nn(jnp.concatenate(att_parts, 1), grads)
-
-
-def put_gq(s, offset):
+            scores = nn(k_all[:nj], padded(q_t[head_rows(h), cols], h))
+            blocks = []
+            for half in range(2):
+                ib = 2 * chunk + half
+                lanes = slice(BLOCK * half, BLOCK * half + BLOCK)
+                pieces = []
+                for jb in range(ib):
+                    bias = jnp.where(lay[h, ib, jb] == 1, 0.0, NEG)
+                    pieces.append(scores[BLOCK * jb : BLOCK * jb + BLOCK, lanes] + bias)
+                pieces.append(jnp.where(tri, scores[BLOCK * ib : BLOCK * ib + BLOCK, lanes], NEG))
+                blocks.append(soften(pieces))
+            wts = jnp.concatenate([stacked(x, nj) for x in blocks], 1)
+            product = nn(with_ones(v_t[head_rows(h), :nj]), wts)
+            inv = 1.0 / product[HEAD : HEAD + 1]
+            out = product[:HEAD] * inv
+            dts = (d_t[head_rows(h), cols] * inv).astype(BF)
+            delta = jnp.sum(out * dts.astype(F32), axis=0, keepdims=True)
+            d_prob = nn(v_all[:nj], padded(dts, h))
+            ds_blocks = []
+            for half in range(2):
+                lanes = slice(BLOCK * half, BLOCK * half + BLOCK)
+                ds_blocks.append([
+                    (x.astype(F32) * (d_prob[BLOCK * j : BLOCK * j + BLOCK, lanes] - delta[:, lanes])).astype(BF)
+                    for j, x in enumerate(blocks[half])
+                ])
+            ds = jnp.concatenate([stacked(x, nj) for x in ds_blocks], 1)
+            dqs.append(nn(k_t[head_rows(h), :nj], ds) * SCALE)
+            weights.append(wts)
+            ds_all.append(ds)
+            outs.append(out)
+            dts_all.append(dts)
+        att_t = jnp.concatenate(outs, 0).astype(BF)
+        s["att_row_t"][r, :, cols] = att_t
+        s["att_row"][r, cols] = nt(ident, att_t).astype(BF)
+        dq = nt(ident, jnp.concatenate(dqs, 0).astype(BF)).astype(BF)
+        chunks.append((
+            jnp.concatenate(weights, 1), by_head(turned(jnp.concatenate(dts_all, 0), ident)),
+            jnp.concatenate(ds_all, 1), by_head(q_all[cols]), dq,
+        ))
+    first, second = chunks
+    dv_low = nn(second[0][:width], second[1]) + nn(first[0], first[1])
+    dk_low = nn(second[2][:width], second[3]) + nn(first[2], first[3])
+    dv = jnp.concatenate([dv_low, nn(second[0][width:], second[1])], 0).astype(BF)
+    dk = (jnp.concatenate([dk_low, nn(second[2][width:], second[3])], 0) * SCALE).astype(BF)
+    d_proj = jnp.concatenate([jnp.concatenate([first[4], second[4]], 0), dk, dv], 1)
+    s["dp_row"][r] = d_proj
+    s["gf_row"][r] = nt(d_proj, w)
+
+
+def weight_grads(feats_t, d_proj, put):
     for i in range(3):
-        part = s["gq_acc"][:, i * HALF : (i + 1) * HALF].astype(BF)
-        s["gq"]["g"][:, :, :, :, i * 512 + offset : i * 512 + offset + HALF] = part.reshape(
-            N_Y, N_Z, N_X, 8, HALF
-        )
-
-
-def put_gwo(s, half):
-    part = s["gwo_acc"][...].astype(BF)
-    s["gwo"]["g"][half] = part.reshape(N_Z, N_X, 8, 512)
+        put(i, nn(feats_t, d_proj[:, i * HALF : (i + 1) * HALF]).astype(BF))
+
+
+def put_block(ref, i, part):
+    ref[:, :, :, :, i * HALF : (i + 1) * HALF] = part.reshape(N_Y, N_Z, N_X, 8, HALF)
+
+
+def col_forward(s, c, w, mask, ident):
+    qkv = nn(s["f_col"][c], w).astype(BF)
+    s["qkv"][c] = qkv
+    q_all, k_all, v_all = (qkv[:, i * HALF : (i + 1) * HALF] for i in range(3))
+    q_t, v_t = turned(q_all, ident), turned(v_all, ident)
+    outs = []
+    for h in range(4):
+        scores = nn(k_all, padded(q_t[head_rows(h)], h))
+        early = soften([jnp.where(mask, scores[:BLOCK, :BLOCK], NEG)])
+        late = soften([scores[:BLOCK, BLOCK:], jnp.where(mask, scores[BLOCK:, BLOCK:], NEG)])
+        wts = jnp.concatenate([stacked(early, 256), stacked(late, 256)], 1)
+        s["wts"][c, :, 256 * h : 256 * h + 256] = wts
+        product = nn(with_ones(v_t[head_rows(h)]), wts)
+        inv = 1.0 / product[HEAD : HEAD + 1]
+        s["inv"][c, h : h + 1] = inv
+        outs.append(product[:HEAD] * inv)
+    out = jnp.concatenate(outs, 0)
+    s["o"][c] = out
+    s["a_col"][c] = nt(ident, out.astype(BF)).astype(BF)
+
+
+def col_backward(s, c, w, mask, ident):
+    qkv = s["qkv"][c]
+    q_all, k_all, v_all = (qkv[:, i * HALF : (i + 1) * HALF] for i in range(3))
+    k_t, d_t = turned(k_all, ident), nt(ident, s["d_col"][c])
+    dqs, dts_all, ds_all = [], [], []
+    for h in range(4):
+        dts = (d_t[head_rows(h)] * s["inv"][c, h : h + 1]).astype(BF)
+        delta = jnp.sum(s["o"][c, head_rows(h)] * dts.astype(F32), axis=0, keepdims=True)
+        d_prob = nn(v_all, padded(dts, h))
+
+        def grad(j, i):
+            rows, lanes = slice(BLOCK * j, BLOCK * j + BLOCK), slice(BLOCK * i, BLOCK * i + BLOCK)
+            wts = s["wts"][c, rows, 256 * h + BLOCK * i : 256 * h + BLOCK * i + BLOCK]
+            return (wts.astype(F32) * (d_prob[rows, lanes] - delta[:, lanes])).astype(BF)
+
+        ds = jnp.concatenate([stacked([grad(0, 0)], 256), stacked([grad(0, 1), grad(1, 1)], 256)], 1)
+        dqs.append(nn(k_t[head_rows(h)], ds) * SCALE)
+        dts_all.append(dts)
+        ds_all.append(ds)
+    dq = nt(ident, jnp.concatenate(dqs, 0).astype(BF)).astype(BF)
+    dv = nn(s["wts"][c], by_head(turned(jnp.concatenate(dts_all, 0), ident))).astype(BF)
+    dk = (nn(jnp.concatenate(ds_all, 1), by_head(q_all)) * SCALE).astype(BF)
+    d_proj = jnp.concatenate([dq, dk, dv], 1)
+    s["dp_col"][c] = d_proj
+    s["g_col"][c] = nt(d_proj, w).astype(BF)
 
 
 def whole_kernel(lay, feats, grads, w, wo, out, gf_out, gq_out, gwo_out, s):
@@ -374,97 +456,81 @@
     d_swap.start()
 
     ident = eye(256)
-    s["gq_acc"][...] = jnp.zeros_like(s["gq_acc"])
-    s["gwo_acc"][...] = jnp.zeros_like(s["gwo_acc"])
+    s["w_row"][...] = side_by_side(w, 0)
+    s["w_col"][...] = side_by_side(w, HALF)
+    w_row, w_col = s["w_row"], s["w_col"]
 
     @pl.loop(0, 2)
     def _(r):
-        row_heads(s, r, lay, feats[r], grads[r], w, wo, ident)
-
-    put_gq(s, 0)
-    put_gwo(s, 0)
-
-    key = lax.broadcasted_iota(jnp.int32, (256, 256), 0)
-    qry = lax.broadcasted_iota(jnp.int32, (256, 256), 1)
-    mask = key <= qry
-    wq, wk, wv = (w[:, i * 512 + HALF : i * 512 + 512] for i in range(3))
+        row_heads(s, r, lay, feats[r], grads[r], w_row[...], wo, ident)
+
+    gq_row, gq_col, gwo = (Scatter(p, s[k]["g"], s[k]["bufs"], s[k]["sems"]) for k in ("gq_row", "gq_col", "gwo"))
+    feats_t = jnp.concatenate([turned_wide(feats[r], ident) for r in range(2)], 1)
+    weight_grads(feats_t, s["dp_row"][...].reshape(1024, 768), lambda i, x: put_block(gq_row.g, i, x))
+    gq_row.to_core()
+    part = nn(s["att_row_t"][0], grads[0]) + nn(s["att_row_t"][1], grads[1])
+    gwo.g[0] = part.astype(BF).reshape(N_Z, N_X, 8, 512)
+
+    mask = lax.broadcasted_iota(jnp.int32, (BLOCK, BLOCK), 0) <= lax.broadcasted_iota(
+        jnp.int32, (BLOCK, BLOCK), 1
+    )
     split, join = column_matrix(), uncolumn_matrix()
     f_swap.arrived()
     to_columns(s["f_got"], s["f_col"], split)
 
     @pl.loop(0, 4)
     def _(c):
-        x = s["f_col"][c]
-        q_all = nn(x, wq).astype(BF)
-        k_all = nn(x, wk).astype(BF)
-        v_all = nn(x, wv).astype(BF)
-        s["q"][c], s["k"][c], s["v"][c] = q_all, k_all, v_all
-        q_t, v_t = turned(q_all, ident), turned(v_all, ident)
-        outs = []
-        for h in range(4):
-            probs = softmax_t(nn(k_all, rows_of_head(q_t, h)), mask)
-            s["probs"][c, h] = probs
-            outs.append(nn(v_t[head_rows(h)], probs.astype(BF)))
-        s["a_col"][c] = nt(ident, jnp.concatenate(outs, 0).astype(BF)).astype(BF)
+        col_forward(s, c, w_col[...], mask, ident)
 
     from_columns(s["a_col"], s["a_wire"], join)
+    gq_row.to_x()
     a_swap.start()
 
     d_swap.arrived()
     to_columns(s["d_got"], s["d_col"], split)
-    s["gq_acc"][...] = jnp.zeros_like(s["gq_acc"])
 
     @pl.loop(0, 4)
     def _(c):
-        x = s["f_col"][c]
-        q_all, k_all, v_all, d_all = s["q"][c], s["k"][c], s["v"][c], s["d_col"][c]
-        k_t, d_t = turned(k_all, ident), turned(d_all, ident)
-        dqs, dk, dv = [], None, None
-        for h in range(4):
-            probs = s["probs"][c, h]
-            ds_low = score_grad(probs, nn(v_all, rows_of_head(d_t, h)))
-            dqs.append(nn(k_t[head_rows(h)], ds_low) * SCALE)
-            dv_h = nn(probs.astype(BF), lanes_of_head(d_all, h))
-            dk_h = nn(ds_low, lanes_of_head(q_all, h))
-            dk = dk_h if dk is None else dk + dk_h
-            dv = dv_h if dv is None else dv + dv_h
-        dq = nt(ident, jnp.concatenate(dqs, 0).astype(BF)).astype(BF)
-        dk = (dk * SCALE).astype(BF)
-        dv = dv.astype(BF)
-        s["g_col"][c] = (nt(dq, wq) + nt(dk, wk) + nt(dv, wv)).astype(BF)
-        x_t = turned_wide(x, ident)
-        for i, d in enumerate((dq, dk, dv)):
-            s["gq_acc"][:, i * HALF : (i + 1) * HALF] += nn(x_t, d)
+        col_backward(s, c, w_col[...], mask, ident)
 
     from_columns(s["g_col"], s["g_wire"], join)
+    gq_row.to_y()
     g_swap.start()
-    put_gq(s, HALF)
-    gq = Scatter(p, s["gq"]["g"], s["gq"]["bufs"], s["gq"]["sems"])
-    gwo = Scatter(p, s["gwo"]["g"], s["gwo"]["bufs"], s["gwo"]["sems"])
-    gq.to_core()
+    gq_row.to_z()
+    feats_t = jnp.concatenate([turned_wide(s["f_col"][c], ident) for c in range(4)], 1)
+    weight_grads(feats_t, s["dp_col"][...].reshape(1024, 768), lambda i, x: put_block(gq_col.g, i, x))
+    gq_col.to_core()
 
     unwire = unwire_matrix()
+    gq_row.to_mate()
     a_swap.arrived()
-    s["gwo_acc"][...] = jnp.zeros_like(s["gwo_acc"])
+    part = None
     for b in range(4):
         x = s["a_got"][32 * b : 32 * b + 32]
         a = nn(unwire, x.reshape(256, HALF)).astype(BF)
-        s["gwo_acc"][...] += nn(turned(a, ident), block_of(grads, b))
+        term = nn(turned(a, ident), block_of(grads, b))
+        part = term if part is None else part + term
         s["att_col"][0, 128 * b : 128 * b + 128] = a[:128]
         s["att_col"][1, 128 * b : 128 * b + 128] = a[128:]
-    put_gwo(s, 1)
+    gwo.g[1] = part.astype(BF).reshape(N_Z, N_X, 8, 512)
     gwo.to_core()
-    gq.to_x()
+    gq_col.to_x()
     for r in range(2):
-        out[r] = (nn(s["att_row"][r], wo[:HALF]) + nn(s["att_col"][r], wo[HALF:])).astype(BF)
+        both = jnp.concatenate([s["att_row"][r], s["att_col"][r]], 1)
+        out[r] = nn(both, wo[...]).astype(BF)
     gwo.to_x()
-    gq.to_y()
+    rows = gq_row.result()
+    for i in range(3):
+        gq_out[:, i * 512 : i * 512 + HALF] = rows[:, i * HALF : (i + 1) * HALF]
+    gq_col.to_y()
     gwo.to_y()
-    gq.to_z()
+    gq_col.to_z()
     gwo.to_z()
-    gq.to_mate()
+    gq_col.to_mate()
     gwo.to_mate()
-    gq_out[...] = gq.result()
+    rows = gq_col.result()
+    for i in range(3):
+        gq_out[:, i * 512 + HALF : i * 512 + 512] = rows[:, i * HALF : (i + 1) * HALF]
     gwo_out[...] = gwo.result()
 
     g_swap.arrived()
@@ -493,22 +559,24 @@
         g_wire=vmem((n_ctx, 8, 512), BF),
         g_got=vmem((n_ctx, 8, 512), BF),
         swap=pltpu.SemaphoreType.DMA((8,)),
-        dk=vmem((512, 256), F32),
-        dv=vmem((512, 256), F32),
+        w_row=vmem((512, 768), BF),
+        w_col=vmem((512, 768), BF),
         att_row=vmem((2, 512, 256), BF),
+        att_row_t=vmem((2, 256, 512), BF),
         att_col=vmem((2, 512, 256), BF),
         gf_row=vmem((2, 512, 512), F32),
-        gq_acc=vmem((512, 768), F32),
-        gwo_acc=vmem((256, 512), F32),
+        dp_row=vmem((2, 512, 768), BF),
         f_col=vmem((4, 256, 512), BF),
         d_col=vmem((4, 256, 256), BF),
         a_col=vmem((4, 256, 256), BF),
         g_col=vmem((4, 256, 512), BF),
-        q=vmem((4, 256, 256), BF),
-        k=vmem((4, 256, 256), BF),
-        v=vmem((4, 256, 256), BF),
-        probs=vmem((4, 4, 256, 256), F32),
-        gq=scatter_scratch(1536),
+        qkv=vmem((4, 256, 768), BF),
+        wts=vmem((4, 256, 1024), BF),
+        inv=vmem((4, 8, 256), F32),
+        o=vmem((4, 256, 256), F32),
+        dp_col=vmem((4, 256, 768), BF),
+        gq_row=scatter_scratch(768),
+        gq_col=scatter_scratch(768),
         gwo=scatter_scratch(512),
     )
     flat, tree = jax.tree.flatten(scratch, is_leaf=lambda x: not isinstance(x, (dict, list)))

time: 111 us -> 119 us (1.072)
  Pallas kernels: 106 us -> 114 us
    pallas_call x1, Pallas kernels: 106 us -> 114 us  [on_device(): pl.pallas_call(kernel, out_shape=[jax.ShapeDtypeStruct(shape, BF), jax.Sh...]
where the time goes in v3:
time: 119 us
  Pallas kernels  114 us (96%)
  local copies, waits for them, and re-layouts  4.54 us (4%)
    pallas_call x1, Pallas kernels, on_device(): pl.pallas_call(kernel, out_shape=[jax.ShapeDtypeStruct(shape, BF), jax.Sh...  114 us
    unnamed x10, local copies, waits for them, and re-layouts  4.54 us

profile of v3, /device:TPU:1, one launch (start us, length us, event | category | flops | bytes accessed | tf_op | source)
XLA Modules:
  0.0 118.7 jit_solution(14710944829350387261)
XLA Ops:
  0.6 113.5 %whole_layer.1 = (bf16[2,512,512]{2,1,0:T(8,128)(2,1)}, bf16[2,512,512]{2,1,0:T(8,128)(2,1)}, f32[4,1536]{1,0:T(4,128)}, f32[4,512]{1,0:T(4,128)}) custom-call(s32[4,4,4]{2,1,0:T(4,128)} %lay.1, bf16[2,512,512]{2,1,0:T(8,128)(2,1)} %bitcast.6, bf16[2,512,512]{2,1,0:T(8,128)(2,1)} %bitcast.7, bf16[512,1536]{1,0:T(8,128)(2,1)} %w.1, bf16[512,512]{1,0:T(8,128)(2,1)} %wo.1), custom_call_target="tpu_custom_call" | custom-call | tf_op jit(solution)/shard_map/whole_layer/pallas_call | solution.py:590
  114.2 0.0 copy-start
  114.2 0.0 copy-start.1
  114.2 2.3 %copy.13 = bf16[1,2,512,512]{3,2,1,0:T(8,128)(2,1)} copy(bf16[1,2,512,512]{3,2,1,0:T(8,128)(2,1)} %bitcast.5) | data formatting | bytes 2097152
  116.5 0.0 copy-done
  116.5 0.0 copy-start.2
  116.5 1.0 copy.14
  117.5 0.0 copy-done.1
  117.5 0.6 copy.15
  118.1 0.0 copy-done.2
  118.1 0.6 copy.16
Async XLA Ops:
  114.2 2.4 %copy-start = (bf16[2,512,512]{2,1,0:T(8,128)(2,1)S(1)}, bf16[2,512,512]{2,1,0:T(8,128)(2,1)}, u32[]{:S(2)}) copy-start(bf16[2,512,512]{2,1,0:T(8,128)(2,1)} %get-tuple-element.9) | copy-start | bytes 3145732
  114.2 3.3 %copy-start.1 = (f32[4,1536]{1,0:T(4,128)S(1)}, f32[4,1536]{1,0:T(4,128)}, u32[]{:S(2)}) copy-start(f32[4,1536]{1,0:T(4,128)} %get-tuple-element.18) | copy-start | bytes 73732
  116.5 1.6 %copy-start.2 = (f32[4,512]{1,0:T(4,128)S(1)}, f32[4,512]{1,0:T(4,128)}, u32[]{:S(2)}) copy-start(f32[4,512]{1,0:T(4,128)} %get-tuple-element.19) | copy-start | bytes 24580

commit v4 on v3

--- a/solution.py
+++ b/solution.py
@@ -15,7 +15,7 @@
 NEG = -1e30
 BF = jnp.bfloat16
 F32 = jnp.float32
-VMEM_LIMIT = 58 * 1024 * 1024
+VMEM_LIMIT = 58*1024*1024
 MESH = pl.DeviceIdType.MESH
 N_Y, N_Z, N_X = 2, 8, 4
 SCALE_LOG2E = SCALE * 1.4426950408889634
@@ -428,8 +428,15 @@
     s["g_col"][c] = nt(d_proj, w).astype(BF)
 
 
-def whole_kernel(lay, feats, grads, w, wo, out, gf_out, gq_out, gwo_out, s):
+def whole_kernel(lay, feats_in, grads_in, w_in, wo_in, out, gf_out, gq_out, gwo_out, s):
     p = Place()
+    feats, grads, w, wo = s["feats"], s["grads"], s["w"], s["wo"]
+    loads = [
+        pltpu.make_async_copy(src, dst, s["loads"].at[i])
+        for i, (src, dst) in enumerate(((feats_in, feats), (wo_in, wo), (grads_in, grads), (w_in, w)))
+    ]
+    for load in loads:
+        load.start()
     n_ctx = s["f_wire"].shape[0]
     barrier = pltpu.get_barrier_semaphore()
 
@@ -444,6 +451,7 @@
         pl.semaphore_signal(barrier, inc=1, device_id=p.at(yh=yh, dp=1 - p.dp), device_id_type=MESH)
 
     perm = wire_matrix()
+    loads[0].wait()
     to_wire(s["f_wire"], lambda b: block_of(feats, b), perm)
     pl.semaphore_wait(barrier, n_ctx + 1)
     sems = s["swap"]
@@ -452,6 +460,8 @@
     a_swap = Swap(p, s["a_wire"], s["a_got"], sems.at[4], sems.at[5])
     g_swap = Swap(p, s["g_wire"], s["g_got"], sems.at[6], sems.at[7])
     f_swap.start()
+    for load in loads[1:]:
+        load.wait()
     to_wire(s["d_wire"], lambda b: nt(block_of(grads, b), wo[HALF:]).astype(BF), perm)
     d_swap.start()
 
@@ -483,8 +493,8 @@
         col_forward(s, c, w_col[...], mask, ident)
 
     from_columns(s["a_col"], s["a_wire"], join)
+    a_swap.start()
     gq_row.to_x()
-    a_swap.start()
 
     d_swap.arrived()
     to_columns(s["d_got"], s["d_col"], split)
@@ -494,15 +504,13 @@
         col_backward(s, c, w_col[...], mask, ident)
 
     from_columns(s["g_col"], s["g_wire"], join)
+    g_swap.start()
     gq_row.to_y()
-    g_swap.start()
-    gq_row.to_z()
     feats_t = jnp.concatenate([turned_wide(s["f_col"][c], ident) for c in range(4)], 1)
     weight_grads(feats_t, s["dp_col"][...].reshape(1024, 768), lambda i, x: put_block(gq_col.g, i, x))
     gq_col.to_core()
 
     unwire = unwire_matrix()
-    gq_row.to_mate()
     a_swap.arrived()
     part = None
     for b in range(4):
@@ -519,21 +527,15 @@
         both = jnp.concatenate([s["att_row"][r], s["att_col"][r]], 1)
         out[r] = nn(both, wo[...]).astype(BF)
     gwo.to_x()
-    rows = gq_row.result()
-    for i in range(3):
-        gq_out[:, i * 512 : i * 512 + HALF] = rows[:, i * HALF : (i + 1) * HALF]
+    gq_row.to_z()
     gq_col.to_y()
     gwo.to_y()
     gq_col.to_z()
     gwo.to_z()
-    gq_col.to_mate()
-    gwo.to_mate()
-    rows = gq_col.result()
-    for i in range(3):
-        gq_out[:, i * 512 + HALF : i * 512 + 512] = rows[:, i * HALF : (i + 1) * HALF]
-    gwo_out[...] = gwo.result()
 
     g_swap.arrived()
+    for kind in (gq_row, gq_col, gwo):
+        kind.to_mate()
     for b in range(4):
         x = s["g_got"][32 * b : 32 * b + 32]
         g = nn(unwire, x.reshape(256, 512))
@@ -542,6 +544,11 @@
             gf_out[r, rows] = (s["gf_row"][r, rows] + g[128 * r : 128 * r + 128]).astype(BF)
     for swap in (f_swap, d_swap, a_swap, g_swap):
         swap.gone()
+    for offset, kind in ((0, gq_row), (HALF, gq_col)):
+        rows = kind.result()
+        for i in range(3):
+            gq_out[:, i * 512 + offset : i * 512 + offset + HALF] = rows[:, i * HALF : (i + 1) * HALF]
+    gwo_out[...] = gwo.result()
 
 
 def on_device(features, w_qkv, w_out, layout, grad_out):
@@ -559,6 +566,11 @@
         g_wire=vmem((n_ctx, 8, 512), BF),
         g_got=vmem((n_ctx, 8, 512), BF),
         swap=pltpu.SemaphoreType.DMA((8,)),
+        feats=vmem((2, 512, 512), BF),
+        grads=vmem((2, 512, 512), BF),
+        w=vmem((512, 1536), BF),
+        wo=vmem((512, 512), BF),
+        loads=pltpu.SemaphoreType.DMA((4,)),
         w_row=vmem((512, 768), BF),
         w_col=vmem((512, 768), BF),
         att_row=vmem((2, 512, 256), BF),
@@ -595,7 +607,7 @@
             jax.ShapeDtypeStruct((4, 1536), F32),
             jax.ShapeDtypeStruct((4, 512), F32),
         ],
-        in_specs=[pl.BlockSpec(memory_space=pltpu.SMEM), vm, vm, vm, vm],
+        in_specs=[pl.BlockSpec(memory_space=pltpu.SMEM)] + [pl.BlockSpec(memory_space=pltpu.HBM)] * 4,
         out_specs=[vm] * n_out,
         scratch_shapes=flat,
         compiler_params=pltpu.CompilerParams(

time: 119 us -> 102 us (0.86)
  Pallas kernels: 114 us -> 96.3 us
    pallas_call x1, Pallas kernels: 114 us -> 96.3 us  [on_device(): pl.pallas_call(kernel, out_shape=[jax.ShapeDtypeStruct(shape, BF), jax.Sh...]
where the time goes in v4:
time: 102 us
  Pallas kernels  96.3 us (94%)
  local copies, waits for them, and re-layouts  4.54 us (4%)
    pallas_call x1, Pallas kernels, on_device(): pl.pallas_call(kernel, out_shape=[jax.ShapeDtypeStruct(shape, BF), jax.Sh...  96.3 us
    unnamed x10, local copies, waits for them, and re-layouts  4.54 us

profile of v4, /device:TPU:1, one launch (start us, length us, event | category | flops | bytes accessed | tf_op | source)
XLA Modules:
  0.0 101.5 jit_solution(11345496242878620404)
XLA Ops:
  0.6 96.3 %whole_layer.1 = (bf16[2,512,512]{2,1,0:T(8,128)(2,1)}, bf16[2,512,512]{2,1,0:T(8,128)(2,1)}, f32[4,1536]{1,0:T(4,128)}, f32[4,512]{1,0:T(4,128)}) custom-call(s32[4,4,4]{2,1,0:T(4,128)} %lay.1, bf16[2,512,512]{2,1,0:T(8,128)(2,1)} %bitcast.6, bf16[2,512,512]{2,1,0:T(8,128)(2,1)} %bitcast.7, bf16[512,1536]{1,0:T(8,128)(2,1)} %w.1, bf16[512,512]{1,0:T(8,128)(2,1)} %wo.1), custom_call_target="tpu_custom_call" | custom-call | tf_op jit(solution)/shard_map/whole_layer/pallas_call | solution.py:602
  97.0 0.0 copy-start
  97.0 0.0 copy-start.1
  97.0 2.3 %copy.13 = bf16[1,2,512,512]{3,2,1,0:T(8,128)(2,1)} copy(bf16[1,2,512,512]{3,2,1,0:T(8,128)(2,1)} %bitcast.5) | data formatting | bytes 2097152
  99.3 0.0 copy-done
  99.3 0.0 copy-start.2
  99.3 1.0 copy.14
  100.3 0.0 copy-done.1
  100.3 0.6 copy.15
  100.9 0.0 copy-done.2
  100.9 0.6 copy.16
Async XLA Ops:
  97.0 2.4 %copy-start = (bf16[2,512,512]{2,1,0:T(8,128)(2,1)S(1)}, bf16[2,512,512]{2,1,0:T(8,128)(2,1)}, u32[]{:S(2)}) copy-start(bf16[2,512,512]{2,1,0:T(8,128)(2,1)} %get-tuple-element.9) | copy-start | bytes 3145732
  97.0 3.3 %copy-start.1 = (f32[4,1536]{1,0:T(4,128)S(1)}, f32[4,1536]{1,0:T(4,128)}, u32[]{:S(2)}) copy-start(f32[4,1536]{1,0:T(4,128)} %get-tuple-element.18) | copy-start | bytes 73732
  99.3 1.6 %copy-start.2 = (f32[4,512]{1,0:T(4,128)S(1)}, f32[4,512]{1,0:T(4,128)}, u32[]{:S(2)}) copy-start(f32[4,512]{1,0:T(4,128)} %get-tuple-element.19) | copy-start | bytes 24580

commit v5 on v4

--- a/solution.py
+++ b/solution.py
@@ -15,7 +15,7 @@
 NEG = -1e30
 BF = jnp.bfloat16
 F32 = jnp.float32
-VMEM_LIMIT = 58*1024*1024
+VMEM_LIMIT = 40 * 1024 * 1024
 MESH = pl.DeviceIdType.MESH
 N_Y, N_Z, N_X = 2, 8, 4
 SCALE_LOG2E = SCALE * 1.4426950408889634
@@ -368,7 +368,6 @@
     dk = (jnp.concatenate([dk_low, nn(second[2][width:], second[3])], 0) * SCALE).astype(BF)
     d_proj = jnp.concatenate([jnp.concatenate([first[4], second[4]], 0), dk, dv], 1)
     s["dp_row"][r] = d_proj
-    s["gf_row"][r] = nt(d_proj, w)
 
 
 def weight_grads(feats_t, d_proj, put):
@@ -478,8 +477,6 @@
     feats_t = jnp.concatenate([turned_wide(feats[r], ident) for r in range(2)], 1)
     weight_grads(feats_t, s["dp_row"][...].reshape(1024, 768), lambda i, x: put_block(gq_row.g, i, x))
     gq_row.to_core()
-    part = nn(s["att_row_t"][0], grads[0]) + nn(s["att_row_t"][1], grads[1])
-    gwo.g[0] = part.astype(BF).reshape(N_Z, N_X, 8, 512)
 
     mask = lax.broadcasted_iota(jnp.int32, (BLOCK, BLOCK), 0) <= lax.broadcasted_iota(
         jnp.int32, (BLOCK, BLOCK), 1
@@ -488,9 +485,10 @@
     f_swap.arrived()
     to_columns(s["f_got"], s["f_col"], split)
 
-    @pl.loop(0, 4)
-    def _(c):
-        col_forward(s, c, w_col[...], mask, ident)
+    @pl.loop(0, 2)
+    def _(pair):
+        for c in (2 * pair, 2 * pair + 1):
+            col_forward(s, c, w_col[...], mask, ident)
 
     from_columns(s["a_col"], s["a_wire"], join)
     a_swap.start()
@@ -499,9 +497,10 @@
     d_swap.arrived()
     to_columns(s["d_got"], s["d_col"], split)
 
-    @pl.loop(0, 4)
-    def _(c):
-        col_backward(s, c, w_col[...], mask, ident)
+    @pl.loop(0, 2)
+    def _(pair):
+        for c in (2 * pair, 2 * pair + 1):
+            col_backward(s, c, w_col[...], mask, ident)
 
     from_columns(s["g_col"], s["g_wire"], join)
     g_swap.start()
@@ -509,6 +508,8 @@
     feats_t = jnp.concatenate([turned_wide(s["f_col"][c], ident) for c in range(4)], 1)
     weight_grads(feats_t, s["dp_col"][...].reshape(1024, 768), lambda i, x: put_block(gq_col.g, i, x))
     gq_col.to_core()
+    part = nn(s["att_row_t"][0], grads[0]) + nn(s["att_row_t"][1], grads[1])
+    gwo.g[0] = part.astype(BF).reshape(N_Z, N_X, 8, 512)
 
     unwire = unwire_matrix()
     a_swap.arrived()
@@ -529,6 +530,8 @@
     gwo.to_x()
     gq_row.to_z()
     gq_col.to_y()
+    for r in range(2):
+        s["gf_row"][r] = nt(s["dp_row"][r], w_row[...])
     gwo.to_y()
     gq_col.to_z()
     gwo.to_z()
@@ -614,7 +617,12 @@
             collective_id=1, has_side_effects=True, vmem_limit_bytes=VMEM_LIMIT
         ),
         name="whole_layer",
-    )(layout, features.reshape(shape), grad_out.reshape(shape), w_qkv, w_out)
+    )(
+        *(
+            pltpu.with_memory_space_constraint(a, pltpu.HBM)
+            for a in (layout, features.reshape(shape), grad_out.reshape(shape), w_qkv, w_out)
+        )
+    )
     full = (n_clips,) + shape
     return out.reshape(full), gf.reshape(full), gq, gwo
 

time: 102 us -> 99.1 us (0.972)
  Pallas kernels: 96.3 us -> 94.8 us
  local copies, waits for them, and re-layouts: 4.54 us -> 3.15 us
    pallas_call x1, Pallas kernels: 96.3 us -> 94.8 us  [on_device(): pl.pallas_call(kernel, out_shape=[jax.ShapeDtypeStruct(shape, BF), jax.Sh...]
    unnamed x10 -> x4, local copies, waits for them, and re-layouts: 4.54 us -> 3.15 us
where the time goes in v5:
time: 99.1 us; the launch traced here: 98.6 us
  Pallas kernels  94.8 us (96%)
  local copies, waits for them, and re-layouts  3.15 us (3%)
    pallas_call x1, Pallas kernels, on_device(): pl.pallas_call(kernel, out_shape=[jax.ShapeDtypeStruct(shape, BF), jax.Sh...  94.8 us
    unnamed x4, local copies, waits for them, and re-layouts  3.15 us

profile of v5, /device:TPU:1, one launch (start us, length us, event | category | flops | bytes accessed | tf_op | source)
XLA Modules:
  0.0 98.6 jit_solution(1343717986080602662)
XLA Ops:
  0.6 94.8 %whole_layer.1 = (bf16[2,512,512]{2,1,0:T(8,128)(2,1)S(1)}, bf16[2,512,512]{2,1,0:T(8,128)(2,1)S(1)}, f32[4,1536]{1,0:T(4,128)S(1)}, f32[4,512]{1,0:T(4,128)S(1)}) custom-call(s32[4,4,4]{2,1,0:T(4,128)} %lay.1, bf16[2,512,512]{2,1,0:T(8,128)(2,1)} %bitcast.6, bf16[2,512,512]{2,1,0:T(8,128)(2,1)} %bitcast.7, bf16[512,1536]{1,0:T(8,128)(2,1)} %w.1, ...), custom_call_target="tpu_custom_call" | custom-call | tf_op jit(solution)/shard_map/whole_layer/pallas_call | solution.py:605
  95.4 1.0 copy.13
  96.4 1.0 copy.14
  97.3 0.6 copy.15
  98.0 0.6 copy.16

commit v6 on v5

--- a/solution.py
+++ b/solution.py
@@ -510,6 +510,7 @@
     gq_col.to_core()
     part = nn(s["att_row_t"][0], grads[0]) + nn(s["att_row_t"][1], grads[1])
     gwo.g[0] = part.astype(BF).reshape(N_Z, N_X, 8, 512)
+    gq_col.to_x()
 
     unwire = unwire_matrix()
     a_swap.arrived()
@@ -523,23 +524,23 @@
         s["att_col"][1, 128 * b : 128 * b + 128] = a[128:]
     gwo.g[1] = part.astype(BF).reshape(N_Z, N_X, 8, 512)
     gwo.to_core()
-    gq_col.to_x()
     for r in range(2):
         both = jnp.concatenate([s["att_row"][r], s["att_col"][r]], 1)
         out[r] = nn(both, wo[...]).astype(BF)
     gwo.to_x()
     gq_row.to_z()
-    gq_col.to_y()
     for r in range(2):
         s["gf_row"][r] = nt(s["dp_row"][r], w_row[...])
+    gq_col.to_y()
     gwo.to_y()
     gq_col.to_z()
     gwo.to_z()
 
     g_swap.arrived()
-    for kind in (gq_row, gq_col, gwo):
-        kind.to_mate()
     for b in range(4):
+        if b == 2:
+            for kind in (gq_row, gq_col, gwo):
+                kind.to_mate()
         x = s["g_got"][32 * b : 32 * b + 32]
         g = nn(unwire, x.reshape(256, 512))
         for r in range(2):

time: 99.1 us -> 98.6 us (level)
  no operation moved by 1% of the time
where the time goes in v6:
time: 98.6 us; the launch traced here: 98.5 us
  Pallas kernels  94.7 us (96%)
  local copies, waits for them, and re-layouts  3.15 us (3%)
    pallas_call x1, Pallas kernels, on_device(): pl.pallas_call(kernel, out_shape=[jax.ShapeDtypeStruct(shape, BF), jax.Sh...  94.7 us
    unnamed x4, local copies, waits for them, and re-layouts  3.15 us

profile of v6, /device:TPU:1, one launch (start us, length us, event | category | flops | bytes accessed | tf_op | source)
XLA Modules:
  0.0 98.5 jit_solution(2896729719301059210)
XLA Ops:
  0.6 94.7 %whole_layer.1 = (bf16[2,512,512]{2,1,0:T(8,128)(2,1)S(1)}, bf16[2,512,512]{2,1,0:T(8,128)(2,1)S(1)}, f32[4,1536]{1,0:T(4,128)S(1)}, f32[4,512]{1,0:T(4,128)S(1)}) custom-call(s32[4,4,4]{2,1,0:T(4,128)} %lay.1, bf16[2,512,512]{2,1,0:T(8,128)(2,1)} %bitcast.6, bf16[2,512,512]{2,1,0:T(8,128)(2,1)} %bitcast.7, bf16[512,1536]{1,0:T(8,128)(2,1)} %w.1, ...), custom_call_target="tpu_custom_call" | custom-call | tf_op jit(solution)/shard_map/whole_layer/pallas_call | solution.py:606
  95.4 1.0 copy.13
  96.3 1.0 copy.14
  97.3 0.6 copy.15
  97.9 0.6 copy.16

commit v7 on v6

--- a/solution.py
+++ b/solution.py
@@ -254,11 +254,11 @@
         p, n = self.place, self.n
 
         def step(s, carry):
-            to = (p.ctx + s) % n
+            to = lax.rem(p.ctx + s, n)
             remote(self.src.at[to], self.dst.at[p.ctx], self.send, self.recv, (p.dp, to)).start()
             return carry
 
-        lax.fori_loop(1, n, step, 0)
+        lax.fori_loop(1, n, step, 0, unroll=4)
         self.dst[p.ctx] = self.src[p.ctx]
 
     def all_but_one(self, ref, sem):
@@ -441,11 +441,11 @@
 
     def greet(step, carry):
         pl.semaphore_signal(
-            barrier, inc=1, device_id=(p.dp, (p.ctx + step) % n_ctx), device_id_type=MESH
+            barrier, inc=1, device_id=(p.dp, lax.rem(p.ctx + step, n_ctx)), device_id_type=MESH
         )
         return carry
 
-    lax.fori_loop(1, n_ctx, greet, 0)
+    lax.fori_loop(1, n_ctx, greet, 0, unroll=4)
     for yh in (p.yh, 1 - p.yh):
         pl.semaphore_signal(barrier, inc=1, device_id=p.at(yh=yh, dp=1 - p.dp), device_id_type=MESH)
 

time: 98.6 us -> 98.4 us (level)
  no operation moved by 1% of the time
where the time goes in v7:
time: 98.4 us; the launch traced here: 98.2 us
  Pallas kernels  94.4 us (96%)
  local copies, waits for them, and re-layouts  3.15 us (3%)
    pallas_call x1, Pallas kernels, on_device(): pl.pallas_call(kernel, out_shape=[jax.ShapeDtypeStruct(shape, BF), jax.Sh...  94.4 us
    unnamed x4, local copies, waits for them, and re-layouts  3.15 us

profile of v7, /device:TPU:1, one launch (start us, length us, event | category | flops | bytes accessed | tf_op | source)
XLA Modules:
  0.0 98.2 jit_solution(9653626707798974007)
XLA Ops:
  0.6 94.4 %whole_layer.1 = (bf16[2,512,512]{2,1,0:T(8,128)(2,1)S(1)}, bf16[2,512,512]{2,1,0:T(8,128)(2,1)S(1)}, f32[4,1536]{1,0:T(4,128)S(1)}, f32[4,512]{1,0:T(4,128)S(1)}) custom-call(s32[4,4,4]{2,1,0:T(4,128)} %lay.1, bf16[2,512,512]{2,1,0:T(8,128)(2,1)} %bitcast.6, bf16[2,512,512]{2,1,0:T(8,128)(2,1)} %bitcast.7, bf16[512,1536]{1,0:T(8,128)(2,1)} %w.1, ...), custom_call_target="tpu_custom_call" | custom-call | tf_op jit(solution)/shard_map/whole_layer/pallas_call | solution.py:606
  95.1 1.0 copy.13
  96.1 1.0 copy.14
  97.0 0.6 copy.15
  97.6 0.6 copy.16

commit v8 on v6

--- a/solution.py
+++ b/solution.py
@@ -485,10 +485,9 @@
     f_swap.arrived()
     to_columns(s["f_got"], s["f_col"], split)
 
-    @pl.loop(0, 2)
-    def _(pair):
-        for c in (2 * pair, 2 * pair + 1):
-            col_forward(s, c, w_col[...], mask, ident)
+    @pl.loop(0, 4)
+    def _(c):
+        col_forward(s, c, w_col[...], mask, ident)
 
     from_columns(s["a_col"], s["a_wire"], join)
     a_swap.start()
@@ -497,10 +496,9 @@
     d_swap.arrived()
     to_columns(s["d_got"], s["d_col"], split)
 
-    @pl.loop(0, 2)
-    def _(pair):
-        for c in (2 * pair, 2 * pair + 1):
-            col_backward(s, c, w_col[...], mask, ident)
+    @pl.loop(0, 4)
+    def _(c):
+        col_backward(s, c, w_col[...], mask, ident)
 
     from_columns(s["g_col"], s["g_wire"], join)
     g_swap.start()

time: 98.6 us -> 98.9 us (level)
  no operation moved by 1% of the time
where the time goes in v8:
time: 98.9 us; the launch traced here: 98.8 us
  Pallas kernels  95 us (96%)
  local copies, waits for them, and re-layouts  3.15 us (3%)
    pallas_call x1, Pallas kernels, on_device(): pl.pallas_call(kernel, out_shape=[jax.ShapeDtypeStruct(shape, BF), jax.Sh...  95 us
    unnamed x4, local copies, waits for them, and re-layouts  3.15 us

profile of v8, /device:TPU:1, one launch (start us, length us, event | category | flops | bytes accessed | tf_op | source)
XLA Modules:
  0.0 98.8 jit_solution(9769842389841775433)
XLA Ops:
  0.6 95.0 %whole_layer.1 = (bf16[2,512,512]{2,1,0:T(8,128)(2,1)S(1)}, bf16[2,512,512]{2,1,0:T(8,128)(2,1)S(1)}, f32[4,1536]{1,0:T(4,128)S(1)}, f32[4,512]{1,0:T(4,128)S(1)}) custom-call(s32[4,4,4]{2,1,0:T(4,128)} %lay.1, bf16[2,512,512]{2,1,0:T(8,128)(2,1)} %bitcast.6, bf16[2,512,512]{2,1,0:T(8,128)(2,1)} %bitcast.7, bf16[512,1536]{1,0:T(8,128)(2,1)} %w.1, ...), custom_call_target="tpu_custom_call" | custom-call | tf_op jit(solution)/shard_map/whole_layer/pallas_call | solution.py:604
  95.7 1.0 copy.13
  96.6 1.0 copy.14
  97.6 0.6 copy.15
  98.2 0.6 copy.16
